TPU v7x, 32 devices: a whole 2x2x4 slice. The times are simulated.
32 devices in a mesh: dp: 8 (over z, x), row: 2 (over y), col: 2 (over core).
Axes of the slice: x: 2, y: 2, z: 4, core: 2. Of those that a mesh axis runs over, the one named last changes fastest.
Arguments:
- layer_input: bfloat16 [16384, 768], P(('dp', 'row', 'col')), may hold values from -14 to 14
- encoder_states: bfloat16 [16384, 768], P(('dp', 'row', 'col')), may hold values from -6 to 6
- cotangent: float32 [16384, 768], P(('dp', 'row', 'col')), may hold values from -6 to 6
- buckets: int32 [512], replicated, may hold values from 0 to 31, never falling along the last dimension, each value on 1 to 128 neighbouring positions
- gain_self: float32 [768], P(('row', 'col')), may hold values from 0.5 to 1.5
- gain_cross: float32 [768], P(('row', 'col')), may hold values from 0.5 to 1.5
- gain_ffn: float32 [768], P(('row', 'col')), may hold values from 0.5 to 1.5
- self_query: bfloat16 [768, 768], P('row', 'col'), may hold values from -0.0546875 to 0.0546875
- self_key: bfloat16 [768, 768], P('row', 'col'), may hold values from -0.21875 to 0.21875
- self_value: bfloat16 [768, 768], P('row', 'col'), may hold values from -0.21875 to 0.21875
- self_out: bfloat16 [768, 768], P('col', 'row'), may hold values from -0.625 to 0.625
- cross_query: bfloat16 [768, 768], P('row', 'col'), may hold values from -0.0546875 to 0.0546875
- cross_key: bfloat16 [768, 768], P('row', 'col'), may hold values from -0.21875 to 0.21875
- cross_value: bfloat16 [768, 768], P('row', 'col'), may hold values from -0.21875 to 0.21875
- cross_out: bfloat16 [768, 768], P('col', 'row'), may hold values from -0.625 to 0.625
- ffn_gate: bfloat16 [768, 2048], P('row', 'col'), may hold values from -0.21875 to 0.21875
- ffn_up: bfloat16 [768, 2048], P('row', 'col'), may hold values from -0.21875 to 0.21875
- ffn_down: bfloat16 [2048, 768], P('col', 'row'), may hold values from -0.125 to 0.125
- rel_table: float32 [2, 2, 3, 32], P('col', 'row'), may hold values from -4 to 4
Outputs:
- layer_output: float32 [16384, 768], P(('dp', 'row', 'col'))
- input_grad: float32 [16384, 768], P(('dp', 'row', 'col'))
- encoder_grad: float32 [16384, 768], P(('dp', 'row', 'col'))
- gain_self_grad: float32 [768], P(('row', 'col'))
- gain_cross_grad: float32 [768], P(('row', 'col'))
- gain_ffn_grad: float32 [768], P(('row', 'col'))
- self_query_grad: float32 [768, 768], P('row', 'col')
- self_key_grad: float32 [768, 768], P('row', 'col')
- self_value_grad: float32 [768, 768], P('row', 'col')
- self_out_grad: float32 [768, 768], P('col', 'row')
- cross_query_grad: float32 [768, 768], P('row', 'col')
- cross_key_grad: float32 [768, 768], P('row', 'col')
- cross_value_grad: float32 [768, 768], P('row', 'col')
- cross_out_grad: float32 [768, 768], P('col', 'row')
- ffn_gate_grad: float32 [768, 2048], P('row', 'col')
- ffn_up_grad: float32 [768, 2048], P('row', 'col')
- ffn_down_grad: float32 [2048, 768], P('col', 'row')
- table_grad: float32 [2, 2, 3, 32], P('col', 'row')
Inputs may be any that keep to these rules, and one draw needn't show every extreme that they name: buckets never falls as the distance grows, and each of the 32 buckets is the bucket of some distance.
All inputs are finite; a program needn't handle non-finite values.
Results may differ from a plain program's by a relative error of at most 0.028.
Values may be sent and summed in bfloat16 or wider, within the bound.
No kernel may reach another device: no remote copies, remote signals or barrier semaphores. Data moves between devices by JAX's collectives and lax.ppermute only.
A program may use at most 256 MiB of HBM per device.

v0:
```python
import jax
import jax.numpy as jnp
from jax import lax
from jax.sharding import PartitionSpec as P

D = 768
HD = 64
NB = 32
LEN = 512


epsilon = 1e-06
masked_score = -1e30


def as_sent(x):

    def short(part):
        return part.astype(jnp.bfloat16) if part.dtype == jnp.float32 else part

    return jax.tree.map(short, x)


def gather_columns(operand):
    return lax.all_gather(operand, "col", axis=2, tiled=True)


def gather_rows(operand):
    return jax.tree.map(
        lambda part, own: part.astype(own.dtype),
        lax.all_gather(as_sent(operand), "row", axis=2, tiled=True),
        operand,
    )


def reduce_rows(partial_value):
    return lax.psum_scatter(partial_value, "row", scatter_dimension=2, tiled=True)


def reduce_columns(partial_value):
    return lax.psum_scatter(partial_value, "col", scatter_dimension=2, tiled=True)


def gated(gate_value, up_value):
    return jax.nn.gelu(gate_value, approximate=True) * up_value


def project_up(gathered, stacked):
    flat_weight = stacked.reshape(stacked.shape[0], -1)
    partial_value = jnp.dot(gathered, flat_weight, preferred_element_type=jnp.float32)
    shaped = partial_value.reshape(gathered.shape[0], stacked.shape[1], stacked.shape[2])
    return reduce_rows(shaped)


def project_up_back(gathered, stacked, local_grads):
    whole_grads = gather_rows(local_grads)
    flat_grads = whole_grads.reshape(whole_grads.shape[0], -1)
    flat_weight = stacked.reshape(stacked.shape[0], -1)
    weight_grad = jnp.einsum("td,tw->dw", gathered, flat_grads, preferred_element_type=jnp.float32)
    partial_value = jnp.einsum(
        "tw,dw->td", flat_grads, flat_weight, preferred_element_type=jnp.float32
    )
    input_grad = reduce_columns(partial_value[:, None, :])[:, 0, :]
    return (weight_grad.reshape(stacked.shape), input_grad)


def project_down(local_rows, weight):
    gathered = gather_rows(local_rows[:, None, :])[:, 0, :]
    partial_value = jnp.dot(gathered, weight, preferred_element_type=jnp.float32)
    return (gathered, reduce_columns(partial_value[:, None, :])[:, 0, :])


def project_down_back(gathered, weight, output_grad):
    whole_grads = gather_columns(output_grad.astype(jnp.bfloat16)[:, None, :])[:, 0, :]
    weight_grad = jnp.einsum("tw,td->wd", gathered, whole_grads, preferred_element_type=jnp.float32)
    partial_value = jnp.einsum("td,wd->tw", whole_grads, weight, preferred_element_type=jnp.float32)
    rows_grad = reduce_rows(partial_value[:, None, :])[:, 0, :]
    return (weight_grad, rows_grad)


def normalize(values, gain_values):
    total_sq = lax.psum(jnp.sum(values * values, axis=1, keepdims=True), ("row", "col"))
    rescale = lax.rsqrt(total_sq / D + epsilon)
    normed = gather_columns((values * rescale * gain_values).astype(jnp.bfloat16)[:, None, :])[
        :, 0, :
    ]
    return (normed, rescale)


def normalize_back(values, gain_values, rescale, normed_grad):
    weighted = gain_values * normed_grad
    local_dot = jnp.sum(values * weighted, axis=1, keepdims=True)
    dot_sum = lax.psum(local_dot, ("row", "col"))
    input_grad = rescale * weighted - values * (rescale * rescale * rescale) / D * dot_sum
    gain_grad = jnp.sum(normed_grad * values * rescale, axis=0)
    return (input_grad, gain_grad)


def bias_select(bias_parts, first_row, block_rows, length):
    extended = bias_parts[1]
    reversed_rows = bias_parts[2]
    ahead_rows = lax.dynamic_slice_in_dim(extended, length - 1 - first_row, length, 0)
    behind = lax.dynamic_slice_in_dim(
        reversed_rows, length - first_row - block_rows, block_rows - 1, 0
    )
    return jnp.concatenate([ahead_rows, behind], axis=0)


def block_bias(bias_parts, select, block_rows, length):
    shifted = jnp.dot(
        bias_parts[0], select.T, precision=lax.Precision.HIGHEST, preferred_element_type=jnp.float32
    )
    shift_count = shifted.shape[1]
    tiled_rows = jnp.tile(shifted, (1, block_rows))[:, : block_rows * (shift_count - 1)]
    return tiled_rows.reshape(shifted.shape[0], block_rows, shift_count - 1)[:, :, :length]


def bias_back(score_grads, select, length):
    head_count = score_grads.shape[0]
    block_rows = score_grads.shape[1]
    shift_count = select.shape[0]
    padded = jnp.pad(score_grads, ((0, 0), (0, 0), (0, shift_count - 1 - length)))
    flat_grads = jnp.pad(
        padded.reshape(head_count, block_rows * (shift_count - 1)), ((0, 0), (0, block_rows))
    )
    per_shift = jnp.sum(
        flat_grads.reshape(head_count, block_rows, shift_count), axis=1, dtype=jnp.float32
    )
    return jnp.dot(
        per_shift, select, precision=lax.Precision.HIGHEST, preferred_element_type=jnp.float32
    )


def block_scores(query_block, key_seq, bias_parts, first_row, causal):
    scores = jnp.einsum("qhd,khd->hqk", query_block, key_seq, preferred_element_type=jnp.float32)
    if causal:
        block_rows = query_block.shape[0]
        length = key_seq.shape[0]
        select = bias_select(bias_parts, first_row, block_rows, length)
        scores = scores + block_bias(bias_parts, select, block_rows, length)
        query_pos = first_row + jnp.arange(block_rows, dtype=jnp.int32)
        key_pos = jnp.arange(length, dtype=jnp.int32)
        scores = jnp.where(
            (query_pos[:, None] >= key_pos[None, :])[None, :, :], scores, masked_score
        )
    return scores


def attention_forward(queries, key_rows, value_rows, bias_parts, causal):
    head_count = queries.shape[1] // HD
    sequences = queries.shape[0] // LEN
    length = key_rows.shape[0] // sequences
    block_rows = min(512, LEN)
    blocks = LEN // block_rows
    query_blocks = queries.reshape(sequences * blocks, block_rows, head_count, HD)
    key_seqs = key_rows.reshape(sequences, length, head_count, HD)
    value_seqs = value_rows.reshape(sequences, length, head_count, HD)

    def one_block(block_index):
        scores = block_scores(
            query_blocks[block_index],
            key_seqs[block_index // blocks],
            bias_parts,
            block_index % blocks * block_rows,
            causal,
        )
        maxima = jnp.max(scores, axis=2, keepdims=True)
        shifted = jnp.exp(scores - maxima)
        totals = jnp.sum(shifted, axis=2, keepdims=True)
        weights = (shifted / totals).astype(jnp.bfloat16)
        mixture = jnp.einsum(
            "hqk,khd->qhd",
            weights,
            value_seqs[block_index // blocks],
            preferred_element_type=jnp.float32,
        )
        return (
            mixture.reshape(block_rows, head_count * HD).astype(jnp.bfloat16),
            maxima[:, :, 0] + jnp.log(totals[:, :, 0]),
        )

    mixture, log_totals = lax.map(one_block, jnp.arange(sequences * blocks, dtype=jnp.int32))
    return (mixture.reshape(queries.shape[0], head_count * HD), log_totals)


def attention_backward(queries, key_rows, value_rows, bias_parts, causal, log_totals, output_grads):
    head_count = queries.shape[1] // HD
    sequences = queries.shape[0] // LEN
    length = key_rows.shape[0] // sequences
    block_rows = min(512, LEN)
    blocks = LEN // block_rows
    query_seqs = queries.reshape(sequences, LEN, head_count, HD)
    grad_seqs = output_grads.reshape(sequences, LEN, head_count, HD)
    key_seqs = key_rows.reshape(sequences, length, head_count, HD)
    value_seqs = value_rows.reshape(sequences, length, head_count, HD)
    total_seqs = log_totals.reshape(sequences, blocks, head_count, block_rows)

    def one_sequence(operands):
        query_seq, key_seq, value_seq, total_seq, grad_seq = operands
        bucket_grad = jnp.zeros((head_count, NB), jnp.float32)
        scores = block_scores(query_seq, key_seq, bias_parts, 0, causal)
        weights = jnp.exp(scores - total_seq[0][:, :, None])
        weight_grads = jnp.einsum(
            "qhd,khd->hqk", grad_seq, value_seq, preferred_element_type=jnp.float32
        )
        inner_sum = jnp.sum(weights * weight_grads, axis=2, keepdims=True)
        score_grads = (weights * (weight_grads - inner_sum)).astype(jnp.bfloat16)
        query_grads = [
            jnp.einsum("hqk,khd->qhd", score_grads, key_seq, preferred_element_type=jnp.float32)
        ]
        key_grad = jnp.einsum(
            "hqk,qhd->khd", score_grads, query_seq, preferred_element_type=jnp.float32
        )
        value_grad = jnp.einsum(
            "hqk,qhd->khd",
            weights.astype(jnp.bfloat16),
            grad_seq,
            preferred_element_type=jnp.float32,
        )
        if causal:
            select = bias_select(bias_parts, 0, block_rows, length)
            bucket_grad = bias_back(score_grads, select, length)
        return (jnp.concatenate(query_grads, axis=0), key_grad, value_grad, bucket_grad)

    query_grad, key_grad, value_grad, bucket_grad = lax.map(
        one_sequence, (query_seqs, key_seqs, value_seqs, total_seqs, grad_seqs)
    )
    return (
        query_grad.reshape(queries.shape[0], head_count * HD),
        key_grad.reshape(key_rows.shape[0], head_count * HD),
        value_grad.reshape(key_rows.shape[0], head_count * HD),
        jnp.sum(bucket_grad, axis=0),
    )


def local(
    layer_input,
    encoder_states,
    cotangent,
    buckets,
    gain_self,
    gain_cross,
    gain_ffn,
    self_query,
    self_key,
    self_value,
    self_out,
    cross_query,
    cross_key,
    cross_value,
    cross_out,
    ffn_gate,
    ffn_up,
    ffn_down,
    rel_table,
):
    table_heads_dev = rel_table.shape[2]
    onehot = (buckets[:, None] == jnp.arange(NB, dtype=jnp.int32)[None, :]).astype(jnp.float32)
    reversed_rows = onehot[::-1]
    extended = jnp.concatenate([reversed_rows, jnp.broadcast_to(onehot[0:1], onehot.shape)], axis=0)
    self_local = jnp.stack([self_query, self_key, self_value], axis=1)
    cross_local = jnp.stack([cross_key, cross_value], axis=1)
    query_local = cross_query[:, None, :]
    ffn_local = jnp.stack([ffn_gate, ffn_up], axis=1)
    residual, out_grad, encoder_float = (
        lax.all_to_all(
            layer_input.astype(jnp.float32).astype(jnp.bfloat16),
            ("row", "col"),
            split_axis=1,
            concat_axis=0,
            tiled=True,
        ).astype(jnp.float32),
        lax.all_to_all(
            cotangent.astype(jnp.bfloat16), ("row", "col"), split_axis=1, concat_axis=0, tiled=True
        ).astype(cotangent.dtype),
        lax.all_to_all(
            encoder_states.astype(jnp.float32).astype(jnp.bfloat16),
            ("row", "col"),
            split_axis=1,
            concat_axis=0,
            tiled=True,
        ).astype(jnp.float32),
    )
    encoder_rows = encoder_float.astype(jnp.bfloat16)
    self_stack, cross_stack, query_stack, ffn_stack = (
        self_local,
        cross_local,
        query_local,
        ffn_local,
    )
    self_weight, cross_weight, down_weight = (self_out, cross_out, ffn_down)
    self_gain, cross_gain, ffn_gain = (gain_self, gain_cross, gain_ffn)
    table_heads = rel_table.reshape(table_heads_dev, NB)
    bias_parts = (table_heads, extended, reversed_rows)
    normed_one, rescale_one = normalize(residual, self_gain)
    self_proj = project_up(normed_one, self_stack).astype(jnp.bfloat16)
    self_queries = self_proj[:, 0]
    self_keys = self_proj[:, 1]
    self_values = self_proj[:, 2]
    self_attended, self_totals = attention_forward(
        self_queries, self_keys, self_values, bias_parts, True
    )
    self_gathered, self_branch = project_down(self_attended, self_weight)
    middle = residual + self_branch
    normed_two, rescale_two = normalize(middle, cross_gain)
    cross_queries = project_up(normed_two, query_stack)[:, 0].astype(jnp.bfloat16)
    encoder_whole = gather_columns(encoder_rows[:, None, :])[:, 0, :]
    cross_proj = project_up(encoder_whole, cross_stack).astype(jnp.bfloat16)
    cross_keys = cross_proj[:, 0]
    cross_values = cross_proj[:, 1]
    cross_attended, cross_totals = attention_forward(
        cross_queries, cross_keys, cross_values, bias_parts, False
    )
    cross_gathered, cross_branch = project_down(cross_attended, cross_weight)
    after_cross = middle + cross_branch
    normed_three, rescale_three = normalize(after_cross, ffn_gain)
    gate_up = project_up(normed_three, ffn_stack)
    gate_value = gate_up[:, 0]
    up_value = gate_up[:, 1]
    hidden = gated(gate_value, up_value).astype(jnp.bfloat16)
    hidden_gathered, ffn_branch = project_down(hidden, down_weight)
    layer_output = after_cross + ffn_branch
    down_grad, hidden_grad = project_down_back(hidden_gathered, down_weight, out_grad)
    unused_value, gated_back = jax.vjp(gated, gate_value, up_value)
    gate_grad, up_grad = gated_back(hidden_grad)
    ffn_stack_grad, normed_three_grad = project_up_back(
        normed_three, ffn_stack, jnp.stack([gate_grad, up_grad], axis=1).astype(jnp.bfloat16)
    )
    third_grad, gain_ffn_grad = normalize_back(
        after_cross, ffn_gain, rescale_three, normed_three_grad
    )
    after_grad = out_grad + third_grad
    cross_out_grad, cross_mixed_grad = project_down_back(cross_gathered, cross_weight, after_grad)
    cross_query_rows, cross_key_rows, cross_value_rows, unused_table = attention_backward(
        cross_queries,
        cross_keys,
        cross_values,
        bias_parts,
        False,
        cross_totals,
        cross_mixed_grad.astype(jnp.bfloat16),
    )
    query_stack_grad, normed_two_grad = project_up_back(
        normed_two, query_stack, cross_query_rows.astype(jnp.bfloat16)[:, None, :]
    )
    cross_stack_grad, encoder_grad = project_up_back(
        encoder_whole,
        cross_stack,
        jnp.stack([cross_key_rows, cross_value_rows], axis=1).astype(jnp.bfloat16),
    )
    second_grad, gain_cross_grad = normalize_back(middle, cross_gain, rescale_two, normed_two_grad)
    middle_grad = after_grad + second_grad
    self_out_grad, self_mixed_grad = project_down_back(self_gathered, self_weight, middle_grad)
    self_query_rows, self_key_rows, self_value_rows, bucket_grad = attention_backward(
        self_queries,
        self_keys,
        self_values,
        bias_parts,
        True,
        self_totals,
        self_mixed_grad.astype(jnp.bfloat16),
    )
    self_stack_grad, normed_one_grad = project_up_back(
        normed_one,
        self_stack,
        jnp.stack([self_query_rows, self_key_rows, self_value_rows], axis=1).astype(jnp.bfloat16),
    )
    first_grad, gain_self_grad = normalize_back(residual, self_gain, rescale_one, normed_one_grad)
    input_grad = middle_grad + first_grad
    table_grad = bucket_grad.reshape(rel_table.shape)
    layer_output, input_grad, encoder_grad = (
        lax.all_to_all(
            as_sent(layer_output), ("row", "col"), split_axis=0, concat_axis=1, tiled=True
        ).astype(layer_output.dtype),
        lax.all_to_all(
            as_sent(input_grad), ("row", "col"), split_axis=0, concat_axis=1, tiled=True
        ).astype(input_grad.dtype),
        lax.all_to_all(
            encoder_grad.astype(jnp.bfloat16),
            ("row", "col"),
            split_axis=0,
            concat_axis=1,
            tiled=True,
        ).astype(encoder_grad.dtype),
    )
    grad_list = (
        ffn_stack_grad,
        down_grad,
        gain_ffn_grad,
        query_stack_grad,
        cross_stack_grad,
        cross_out_grad,
        gain_cross_grad,
        self_stack_grad,
        self_out_grad,
        gain_self_grad,
        table_grad,
    )
    flat_grads = jnp.concatenate([member.reshape(-1) for member in grad_list], axis=0)
    dp_count = lax.axis_size("dp")
    total_count = flat_grads.shape[0]
    padding = -total_count % dp_count
    flat_grads = jnp.pad(flat_grads, (0, padding))
    share = lax.psum_scatter(flat_grads, "dp", scatter_dimension=0, tiled=True)
    summed = lax.all_gather(share.astype(jnp.bfloat16), "dp", axis=0, tiled=True).astype(
        share.dtype
    )
    results = []
    offset = 0
    for member in grad_list:
        count = member.size
        results.append(summed[offset : offset + count].reshape(member.shape))
        offset = offset + count
    (
        ffn_stack_sum,
        down_sum,
        gain_ffn_sum,
        query_stack_sum,
        cross_stack_sum,
        cross_out_sum,
        gain_cross_sum,
        self_stack_sum,
        self_out_sum,
        gain_self_sum,
        table_sum,
    ) = results
    return (
        layer_output,
        input_grad,
        encoder_grad,
        gain_self_sum,
        gain_cross_sum,
        gain_ffn_sum,
        self_stack_sum[:, 0],
        self_stack_sum[:, 1],
        self_stack_sum[:, 2],
        self_out_sum,
        query_stack_sum[:, 0],
        cross_stack_sum[:, 0],
        cross_stack_sum[:, 1],
        cross_out_sum,
        ffn_stack_sum[:, 0],
        ffn_stack_sum[:, 1],
        down_sum,
        table_sum,
    )


def solution(mesh):
    in_specs = (
        P(("dp", "row", "col"), None),
        P(("dp", "row", "col"), None),
        P(("dp", "row", "col"), None),
        P(),
        P(("row", "col")),
        P(("row", "col")),
        P(("row", "col")),
        P("row", "col"),
        P("row", "col"),
        P("row", "col"),
        P("col", "row"),
        P("row", "col"),
        P("row", "col"),
        P("row", "col"),
        P("col", "row"),
        P("row", "col"),
        P("row", "col"),
        P("col", "row"),
        P("col", "row", None, None),
    )
    out_specs = (
        P(("dp", "row", "col"), None),
        P(("dp", "row", "col"), None),
        P(("dp", "row", "col"), None),
        P(("row", "col")),
        P(("row", "col")),
        P(("row", "col")),
        P("row", "col"),
        P("row", "col"),
        P("row", "col"),
        P("col", "row"),
        P("row", "col"),
        P("row", "col"),
        P("row", "col"),
        P("col", "row"),
        P("row", "col"),
        P("row", "col"),
        P("col", "row"),
        P("col", "row", None, None),
    )
    return jax.shard_map(local, mesh=mesh, in_specs=in_specs, out_specs=out_specs, check_vma=False)
```

profile of v0, /device:TPU:0, one launch (start us, length us, event | category | flops | bytes accessed | tf_op | source)
XLA Modules:
  0.0 4417.3 jit_solution(11660051140058673260)
XLA Ops:
  8.7 15.7 all_to_all.75
  42.0 8.1 all-gather.15.cloned.1.call-done
  58.5 110.0 %reduce-scatter.5.cloned.1.call-done = f32[2048,3,192]{0,2,1:T(8,128)} async-done(((f32[2048,3,384]{0,2,1:T(8,128)}), f32[2048,3,192]{0,2,1:T(8,128)}) %reduce-scatter.5.cloned.1.call-update) | async-done | bytes 4718608 | tf_op jit(solution)/shard_map/reduce_scatter | solution.py:37
  180.6 209.4 %while.63 = (s32[]{:T(128)}, bf16[4,512,192]{1,2,0:T(8,128)(2,1)}, f32[4,3,512]{2,1,0:T(4,128)S(1)}, s32[4]{0:T(128)S(1)}, bf16[4,512,3,64]{1,3,2,0:T(8,128)(2,1...) while((s32[]{:T(128)}, bf16[4,512,192]{1,2,0:T(8,128)(2,1)}, ...), condition=%wide.region_6.7_spmd, body=%wide.region_3.6_spmd.sunk | while | flops 207976960 | bytes 70915728 | solution.py:182
  186.7 13.4 tile.32
  207.6 13.3 reshape.700
  238.9 13.4 tile.32
  259.8 13.3 reshape.700
  291.2 13.4 tile.32
  312.0 13.3 reshape.700
  343.4 13.4 tile.32
  364.2 13.3 reshape.700
  397.5 19.7 all_to_all.76
  419.3 9.3 all-gather.17.cloned.1.call-done
  432.9 8.7 copy.293
  452.4 14.7 all-reduce.29.cloned.1.call-done
  491.1 56.8 %reduce-scatter.7.cloned.1.call-done = f32[2048,2,192]{0,2,1:T(8,128)} async-done(((f32[2048,2,384]{0,2,1:T(8,128)}), f32[2048,2,192]{0,2,1:T(8,128)}) %reduce-scatter.7.cloned.1.call-update) | async-done | bytes 3145744 | tf_op jit(solution)/shard_map/reduce_scatter | solution.py:37
  564.1 8.6 copy.301
  572.7 571.5 %all-reduce.38 = bf16[2048,1,384]{0,1,2:T(2,128)(2,1)} all-reduce(f32[2048,1,384]{0,1,2:T(1,128)} %copy.301), channel_id=5, replica_groups=mesh['dp'=8,'row'=2,'col'=2] {'row'}, use_global_device_ids=true, to_apply=%region_10.11.clone | all-reduce | flops 786432 | bytes 4718592
  1151.9 23.7 while.64
  1179.4 27.2 all-gather.23.cloned.1.call-done
  1210.8 8.6 copy.307
  1221.2 14.1 all_to_all.77
  1276.8 12.2 fusion.124
  1289.1 87.3 %reduce-scatter.11.cloned.1.call-done = f32[2048,1,512]{2,0,1:T(8,128)} async-done(((f32[2048,1,1024]{2,0,1:T(8,128)}), f32[2048,1,512]{2,0,1:T(8,128)}) %reduce-scatter.11.cloned.1.call-update) | async-done | bytes 4194320 | tf_op jit(solution)/shard_map/reduce_scatter | solution.py:37
  1376.3 191.5 %reduce-scatter.9.cloned.1.call-done = f32[2048,2,512]{2,0,1:T(8,128)} async-done(((f32[2048,2,1024]{2,0,1:T(8,128)}), f32[2048,2,512]{2,0,1:T(8,128)}) %reduce-scatter.9.cloned.1.call-update) | async-done | bytes 8388624 | tf_op jit(solution)/shard_map/reduce_scatter | solution.py:37
  1577.6 104.1 %all-gather.31.cloned.1.call-done = bf16[2048,2,1024]{2,0,1:T(8,128)(2,1)} async-done(((bf16[2048,2,512]{2,0,1:T(8,128)(2,1)}), bf16[2048,2,1024]{2,0,1:T(8,128)(2,1)}) %all-gather.31.cloned.1.call-update) | async-done | bytes 8388624 | tf_op jit(solution)/shard_map/all_gather | solution.py:31
  1681.7 10.0 convolution_bitcast_fusion.13
  1691.8 8.6 copy.316
  1700.6 23.1 all-reduce.33.cloned.1.call-done
  1745.6 9.9 all-gather.33.cloned.1.call-done
  1759.9 8.6 copy.319
  1768.4 571.6 %all-reduce.39 = bf16[2048,1,384]{0,1,2:T(2,128)(2,1)} all-reduce(f32[2048,1,384]{0,1,2:T(1,128)} %copy.319), channel_id=11, replica_groups=mesh['dp'=8,'row'=2,'col'=2] {'row'}, use_global_device_ids=true, to_apply=%region_25.26.clone | all-reduce | flops 786432 | bytes 4718592
  2355.0 34.5 while.65
  2392.9 27.3 all-gather.35.cloned.1.call-done
  2424.5 8.7 copy.326
  2433.2 23.3 all-reduce.35.cloned.1.call-done
  2480.3 9.3 all-gather.37.cloned.1.call-done
  2493.9 8.7 copy.329
  2502.6 609.5 %all-reduce.40 = bf16[2048,1,384]{0,1,2:T(2,128)(2,1)} all-reduce(f32[2048,1,384]{0,1,2:T(1,128)} %copy.329), channel_id=13, replica_groups=mesh['dp'=8,'row'=2,'col'=2] {'row'}, use_global_device_ids=true, to_apply=%region_32.33.clone | all-reduce | flops 786432 | bytes 4718592
  3121.7 438.2 %while.66 = (s32[]{:T(128)}, bf16[4,512,3,64]{1,3,2,0:T(8,128)(2,1)}, bf16[4,512,3,64]{1,3,2,0:T(8,128)(2,1)}, bf16[4,512,3,64]{1,3,2,0:T(8,128)(2,1)}, f32[4,3,...) while((s32[]{:T(128)}, ...), condition=%wide.region_36.37_spmd, body=%wide.region_33.36_spmd.sunk | while | flops 514973056 | bytes 186006896 | solution.py:225
  3148.8 13.4 tile.34
  3169.7 13.4 reshape.701
  3220.7 13.2 reshape.704
  3251.8 13.4 tile.34
  3272.7 13.4 reshape.701
  3323.7 13.2 reshape.704
  3354.8 13.4 tile.34
  3375.6 13.4 reshape.701
  3426.7 13.2 reshape.704
  3457.8 13.4 tile.34
  3478.6 13.4 reshape.701
  3529.6 13.2 reshape.704
  3582.7 9.0 copy.312
  3591.7 42.2 all-gather.39.cloned.1.call-done
  3640.7 8.7 copy.338
  3660.6 11.7 copy.344
  3704.7 9.1 copy.342
  3735.2 76.9 %concatenate.21 = f32[2359968]{0:T(1024)} concatenate(f32[786432]{0:T(1024)} %bitcast.603, f32[393216]{0:T(1024)} %reshape.591, f32[192]{0:T(256)S(1)} %copy-done.81, f32[147456]{0:T(1024)} %reshape_reshape.16, f32[294912]{0:T(1024)} %reshape_reshape.17, f32[147456]{0:T(1024)S(1)} %reshape.593, f32[192]{0:T(256)S(1)} %copy-done.82, f32[442368]{0:T(1024)S(1)} %reshape_reshape.18, ...), dimensions={0} | concatenate | bytes 18879744 | tf_op jit(solution)/shard_map/concatenate | solution.py:399
  3812.0 368.3 %all-reduce.41 = bf16[2359968]{0:T(1024)(128)(2,1)} all-reduce(f32[2359968]{0:T(1024)} %concatenate.21), channel_id=16, replica_groups=mesh['dp'=8,'row'=2,'col'=2] {'dp'}, use_global_device_ids=true, to_apply=%region_45.46.clone | all-reduce | flops 2359968 | bytes 14159808
  4184.4 10.2 dynamic-update-slice
  4194.6 66.3 %all-reduce.42 = bf16[2048,1,384]{0,1,2:T(2,128)(2,1)} all-reduce(f32[2048,1,384]{0,1,2:T(1,128)} %copy.342), channel_id=15, replica_groups=mesh['dp'=8,'row'=2,'col'=2] {'col'}, use_global_device_ids=true, to_apply=%region_40.41.clone | all-reduce | flops 786432 | bytes 4718592
  4294.9 15.9 all_to_all.78
  4328.0 35.5 all-reduce.27.cloned.1.call-done
  (672 shorter events, 848.4 us)
Async XLA Ops:
  7.2 1256.6 %copy-start = (bf16[1024,384]{1,0:T(8,128)(2,1)S(1)}, bf16[1024,384]{1,0:T(8,128)(2,1)}, u32[]{:S(2)}) copy-start(bf16[1024,384]{1,0:T(8,128)(2,1)} %param.44) | copy-start | bytes 2359300
  7.2 42.9 all-gather.15.cloned.1.call-start
  24.4 7.5 copy-start.7
  39.4 129.1 %reduce-scatter.5.cloned.1.call-start = ((), (), s32[]{:S(2)}) async-start(), calls=%async_computation.11 | async-start | bytes 14155776 | tf_op jit(solution)/shard_map/reduce_scatter | solution.py:37
  56.6 372.1 %all-gather.17.cloned.1.call-start = ((), (), s32[]{:S(2)}) async-start(), calls=%async_computation.12 | async-start | bytes 2359296 | tf_op jit(solution)/shard_map/all_gather | solution.py:31
  57.6 110.9 %copy-start.58 = (f32[512,32]{0,1:T(8,128)}, f32[512,32]{0,1:T(8,128)S(1)}, u32[]{:S(2)}) copy-start(f32[512,32]{0,1:T(8,128)S(1)} %rev.3) | copy-start | bytes 196612
  58.0 110.5 %copy-start.60 = (f32[511,32]{0,1:T(8,128)}, f32[511,32]{0,1:T(8,128)S(1)}, u32[]{:S(2)}) copy-start(f32[511,32]{0,1:T(8,128)S(1)} %slice.197) | copy-start | bytes 196228
  58.2 110.3 %copy-start.62 = (f32[512,32]{0,1:T(8,128)}, f32[512,32]{0,1:T(8,128)S(1)}, u32[]{:S(2)}) copy-start(f32[512,32]{0,1:T(8,128)S(1)} %broadcast_in_dim.174) | copy-start | bytes 196612
  389.9 6.1 copy-start.10
  390.0 6.0 copy-start.11
  390.0 6.0 copy-start.27
  390.0 6.0 copy-start.41
  390.0 6.0 copy-start.64
  396.1 47.0 %all-gather.19.cloned.1.call-start = ((), (), s32[]{:S(2)}) async-start(), calls=%async_computation.13 | async-start | bytes 2359296 | tf_op jit(solution)/shard_map/all_gather | solution.py:25
  417.8 10.9 copy-start.46
  419.3 47.9 %all-reduce.29.cloned.1.call-start = ((), (), s32[]{:S(2)}) async-start(), calls=%async_computation.29 | async-start | bytes 6291456
  441.6 106.3 %reduce-scatter.7.cloned.1.call-start = ((), (), s32[]{:S(2)}) async-start(), calls=%async_computation.14 | async-start | bytes 9437184 | tf_op jit(solution)/shard_map/reduce_scatter | solution.py:37
  448.9 110.9 %all-gather.21.cloned.1.call-start = ((), (), s32[]{:S(2)}) async-start(), calls=%async_computation.15 | async-start | bytes 2359296 | tf_op jit(solution)/shard_map/all_gather | solution.py:25
  452.4 21.8 copy-start.13
  474.2 11.4 copy-start.77
  489.8 716.8 %all-gather.23.cloned.1.call-start = ((), (), s32[]{:S(2)}) async-start(), calls=%async_computation.16 | async-start | bytes 2359296 | tf_op jit(solution)/shard_map/all_gather | solution.py:31
  551.8 8.1 copy-start.44
  1177.6 28.9 copy-start.43
  1179.1 63.7 %all-reduce.31.cloned.1.call-start = ((), (), s32[]{:S(2)}) async-start(), calls=%async_computation.30 | async-start | bytes 6291456
  1219.4 44.3 %all-gather.29.cloned.1.call-start = ((), (), s32[]{:S(2)}) async-start(), calls=%async_computation.20 | async-start | bytes 2359296 | tf_op jit(solution)/shard_map/all_gather | solution.py:25
  1238.2 38.6 all-gather.25.cloned.1.call-start
  1249.9 10.7 copy-start.75
  1263.7 112.7 %reduce-scatter.11.cloned.1.call-start = ((), (), s32[]{:S(2)}) async-start(), calls=%async_computation.21 | async-start | bytes 12582912 | tf_op jit(solution)/shard_map/reduce_scatter | solution.py:37
  1270.9 296.9 %reduce-scatter.9.cloned.1.call-start = ((), (), s32[]{:S(2)}) async-start(), calls=%async_computation.18 | async-start | bytes 25165824 | tf_op jit(solution)/shard_map/reduce_scatter | solution.py:37
  1289.0 392.7 %all-gather.31.cloned.1.call-start = ((), (), s32[]{:S(2)}) async-start(), calls=%async_computation.22 | async-start | bytes 12582912 | tf_op jit(solution)/shard_map/all_gather | solution.py:31
  1577.6 146.2 %all-reduce.33.cloned.1.call-start = ((), (), s32[]{:S(2)}) async-start(), calls=%async_computation.31 | async-start | bytes 6291456
  1700.3 55.2 %all-gather.33.cloned.1.call-start = ((), (), s32[]{:S(2)}) async-start(), calls=%async_computation.23 | async-start | bytes 2359296 | tf_op jit(solution)/shard_map/all_gather | solution.py:25
  1723.7 7.2 copy-start.5
  1745.6 674.6 %all-gather.35.cloned.1.call-start = ((), (), s32[]{:S(2)}) async-start(), calls=%async_computation.24 | async-start | bytes 2359296 | tf_op jit(solution)/shard_map/all_gather | solution.py:31
  2391.3 28.9 copy-start.45
  2392.8 63.7 %all-reduce.35.cloned.1.call-start = ((), (), s32[]{:S(2)}) async-start(), calls=%async_computation.32 | async-start | bytes 6291456
  2433.2 56.4 %all-gather.37.cloned.1.call-start = ((), (), s32[]{:S(2)}) async-start(), calls=%async_computation.25 | async-start | bytes 2359296 | tf_op jit(solution)/shard_map/all_gather | solution.py:25
  2456.5 7.2 copy-start.6
  2463.8 9.8 copy-start.18
  2473.6 6.1 copy-start.59
  2473.6 6.1 copy-start.61
  2473.6 6.1 copy-start.63
  2479.6 10.0 copy-start.47
  2479.6 1096.3 %all-gather.27.cloned.1.call-start = ((), (), s32[]{:S(2)}) async-start(), calls=%async_computation.19 | async-start | bytes 6291456 | tf_op jit(solution)/shard_map/all_gather | solution.py:31
  2480.2 1153.7 %all-gather.39.cloned.1.call-start = ((), (), s32[]{:S(2)}) async-start(), calls=%async_computation.26 | async-start | bytes 7077888 | tf_op jit(solution)/shard_map/all_gather | solution.py:31
  3190.5 6.0 copy-start.3
  3293.5 6.0 copy-start.3
  3396.5 6.0 copy-start.3
  3499.5 6.0 copy-start.3
  3569.9 120.7 %all-gather.41.cloned.1.call-start = ((), (), s32[]{:S(2)}) async-start(), calls=%async_computation.27 | async-start | bytes 4718592 | tf_op jit(solution)/shard_map/all_gather | solution.py:31
  3575.9 151.4 %all-reduce.37.cloned.1.call-start = ((), (), s32[]{:S(2)}) async-start(), calls=%async_computation.33 | async-start | bytes 12582912
  3582.7 51.2 %copy-start.49 = (bf16[384,384]{1,0:T(8,128)(2,1)S(1)}, bf16[384,384]{1,0:T(8,128)(2,1)}, u32[]{:S(2)}) copy-start(bf16[384,384]{1,0:T(8,128)(2,1)} %param.36) | copy-start | bytes 884740
  3582.7 51.2 %copy-start.51 = (bf16[384,384]{1,0:T(8,128)(2,1)S(1)}, bf16[384,384]{1,0:T(8,128)(2,1)}, u32[]{:S(2)}) copy-start(bf16[384,384]{1,0:T(8,128)(2,1)} %param.35) | copy-start | bytes 884740
  3582.7 51.2 %copy-start.53 = (bf16[384,384]{1,0:T(8,128)(2,1)S(1)}, bf16[384,384]{1,0:T(8,128)(2,1)}, u32[]{:S(2)}) copy-start(bf16[384,384]{1,0:T(8,128)(2,1)} %param.34) | copy-start | bytes 884740
  3649.6 714.0 %all-reduce.27.cloned.1.call-start = ((), (), s32[]{:S(2)}) async-start(), calls=%async_computation.28 | async-start | bytes 9441280
  3660.5 11.7 copy-start.24
  3704.7 9.1 copy-start.25
  3727.2 7.2 copy-start.14
  3727.2 7.2 copy-start.66
  4267.8 27.1 all-to-all-start.5
  4272.3 5.7 copy-start.8
  4278.0 11.6 copy-start.76
  4278.0 11.6 copy-start.78
  4310.9 15.4 all-to-all-start.2
  (86 other events, 189.4 us)
Sparse Core Ops, SparseCore 0:
  39.5 10.5 all-gather.14
  56.7 111.7 reduce-scatter.4
  396.2 32.4 all-gather.16
  430.7 9.8 all-gather.18
  442.7 24.3 all-reduce.28
  469.4 78.4 reduce-scatter.6
  550.1 9.7 all-gather.20
  1179.3 27.2 all-gather.22
  1219.5 23.1 all-reduce.30
  1244.2 10.9 all-gather.28
  1263.8 9.7 all-gather.24
  1275.9 100.4 reduce-scatter.10
  1378.6 189.1 reduce-scatter.8
  1577.7 104.0 all-gather.30
  1700.5 23.1 all-reduce.32
  1745.7 9.7 all-gather.32
  2392.9 27.2 all-gather.34
  2433.3 23.1 all-reduce.34
  2479.7 9.7 all-gather.36
  2491.0 95.9 all-gather.26
  3570.1 63.7 all-gather.38
  3636.1 44.9 all-gather.40
  3683.8 32.0 all-reduce.36
  4194.7 168.8 all-reduce.26
where the time goes:
time: 4440 us; the launch traced here: 4420 us
  blocking collectives  2300 us (52%)
  local copies, waits for them, and re-layouts  910 us (20%)
  waiting for transfers between devices  798 us (18%)
  matrix products  224 us (5%)
  other arithmetic  116 us (3%)
    unnamed x5, blocking collectives  2190 us
    reduce_scatter x4, waiting for transfers between devices, reduce_rows(): lax.psum_scatter(partial_value, 'row', scatter_dimension=2, tiled=True)  446 us
    all_gather x7, waiting for transfers between devices, gather_rows(): lax.all_gather(as_sent(operand), 'row', axis=2, tiled=True)  210 us
    another operation x16, local copies, waits for them, and re-layouts, block_bias(): jnp.tile(shifted, (1, block_rows))[:, :block_rows * (shift_count - 1)]  135 us
    reshape x8, local copies, waits for them, and re-layouts, block_bias(): tiled_rows.reshape(shifted.shape[0], block_rows, shift_count - 1)  107 us
    unnamed x30, waiting for transfers between devices  102 us
  transfers between devices with their start and end apart: 26, of which 19 were waited for; matrix products, arithmetic and copies ran while one was open for 15% of the time, Pallas kernels for 0%

commit v1 on v0

v1 whole, which is shorter than its diff:
```python
import functools

import jax
import jax.numpy as jnp
from jax import lax
from jax.experimental import pallas as pl
from jax.experimental.pallas import tpu as pltpu
from jax.sharding import PartitionSpec as P

D = 768
HD = 64
NB = 32
LEN = 512
BLK = 128
HALF = D // 2
PAIRS = HALF // (2 * HD)

epsilon = 1e-06
masked_score = -1e30
f32 = jnp.float32
bf16 = jnp.bfloat16
SWAP = [(0, 1), (1, 0)]


def over_row(x):
    return lax.ppermute(x, "row", SWAP)


def over_col(x):
    return lax.ppermute(x, "col", SWAP)


def dot(a, b):
    return jnp.dot(a, b, preferred_element_type=f32)


def dot_t(a, b):
    return lax.dot_general(a, b, (((1,), (1,)), ((), ())), preferred_element_type=f32)


def t_dot(a, b):
    return lax.dot_general(a, b, (((0,), (0,)), ((), ())), preferred_element_type=f32)


def local_order(x, flag, axis):
    first, second = jnp.split(x, 2, axis=axis)
    swapped = jnp.concatenate([second, first], axis=axis)
    return jnp.where(flag == 0, x, swapped)


def causal_mask():
    rows = lax.broadcasted_iota(jnp.int32, (BLK, BLK), 0)
    cols = lax.broadcasted_iota(jnp.int32, (BLK, BLK), 1)
    return rows >= cols


def softmax_rows(scores):
    top = jnp.max(scores, axis=1, keepdims=True)
    shifted = jnp.exp(scores - top)
    total = jnp.sum(shifted, axis=1, keepdims=True)
    return (shifted * (1.0 / total)).astype(bf16)


def self_fwd_kernel(q_ref, k_ref, v_ref, bias_ref, out_ref, probs_ref):
    mask = causal_mask()
    for head in range(2):
        lanes = slice(head * HD, (head + 1) * HD)
        row = jnp.broadcast_to(bias_ref[0, head : head + 1, :], (BLK, LEN))
        bias = pltpu.roll(row, 0, 1, stride=1, stride_axis=0)
        for block in range(LEN // BLK):
            rows = slice(block * BLK, (block + 1) * BLK)
            wide = (block + 1) * BLK
            scores = dot_t(q_ref[rows, lanes], k_ref[:wide, lanes])
            scores = scores + bias[:, LEN - wide :]
            last = jnp.where(mask, scores[:, wide - BLK :], masked_score)
            if block:
                scores = jnp.concatenate([scores[:, : wide - BLK], last], axis=1)
            else:
                scores = last
            probs = softmax_rows(scores)
            probs_ref[head, rows, :wide] = probs
            out_ref[rows, lanes] = dot(probs, v_ref[:wide, lanes]).astype(bf16)


def cross_fwd_kernel(q_ref, k_ref, v_ref, out_ref, probs_ref):
    for head in range(2):
        lanes = slice(head * HD, (head + 1) * HD)
        for block in range(LEN // BLK):
            rows = slice(block * BLK, (block + 1) * BLK)
            scores = dot_t(q_ref[rows, lanes], k_ref[:, lanes])
            probs = softmax_rows(scores)
            probs_ref[head, rows, :] = probs
            out_ref[rows, lanes] = dot(probs, v_ref[:, lanes]).astype(bf16)


def score_grad_of(probs, weight_grads):
    wide = probs.astype(f32)
    mixed = wide * weight_grads
    inner = jnp.sum(mixed, axis=1, keepdims=True)
    return mixed - wide * inner


def shift_sum(total):
    acc = total[:8]
    for first in range(8, BLK, 8):
        acc = acc + pltpu.roll(total[first : first + 8], LEN - first, 1)
    line = lax.broadcasted_iota(jnp.int32, (8, LEN), 0)
    for bit in (1, 2, 4):
        acc = jnp.where((line & bit) != 0, pltpu.roll(acc, LEN - bit, 1), acc)
    return jnp.sum(acc, axis=0, keepdims=True)


def self_bwd_kernel(q_ref, k_ref, v_ref, g_ref, probs_ref, dq_ref, dk_ref, dv_ref, shift_ref, ds_ref):
    for head in range(2):
        lanes = slice(head * HD, (head + 1) * HD)
        total = jnp.zeros((BLK, LEN), f32)
        for block in range(LEN // BLK):
            rows = slice(block * BLK, (block + 1) * BLK)
            wide = (block + 1) * BLK
            weight_grads = dot_t(g_ref[rows, lanes], v_ref[:wide, lanes])
            grads = score_grad_of(probs_ref[head, rows, :wide], weight_grads)
            if wide < LEN:
                total = total + jnp.concatenate([jnp.zeros((BLK, LEN - wide), f32), grads], axis=1)
            else:
                total = total + grads
            short = grads.astype(bf16)
            ds_ref[rows, :wide] = short
            dq_ref[rows, lanes] = dot(short, k_ref[:wide, lanes]).astype(bf16)
        for block in range(LEN // BLK):
            cols = slice(block * BLK, (block + 1) * BLK)
            rest = slice(block * BLK, LEN)
            dk_ref[cols, lanes] = t_dot(ds_ref[rest, cols], q_ref[rest, lanes]).astype(bf16)
            dv_ref[cols, lanes] = t_dot(probs_ref[head, rest, cols], g_ref[rest, lanes]).astype(bf16)
        shift_ref[0, head : head + 1, :] = shift_sum(total)


def cross_bwd_kernel(q_ref, k_ref, v_ref, g_ref, probs_ref, dq_ref, dk_ref, dv_ref, ds_ref):
    for head in range(2):
        lanes = slice(head * HD, (head + 1) * HD)
        for block in range(LEN // BLK):
            rows = slice(block * BLK, (block + 1) * BLK)
            weight_grads = dot_t(g_ref[rows, lanes], v_ref[:, lanes])
            short = score_grad_of(probs_ref[head, rows, :], weight_grads).astype(bf16)
            ds_ref[rows, :] = short
            dq_ref[rows, lanes] = dot(short, k_ref[:, lanes]).astype(bf16)
        dk_ref[:, lanes] = t_dot(ds_ref[...], q_ref[:, lanes]).astype(bf16)
        dv_ref[:, lanes] = t_dot(probs_ref[head], g_ref[:, lanes]).astype(bf16)


def lane_block(first):
    return pl.BlockSpec((LEN, 2 * HD), lambda s, g: (s, first + g))


PROBS = pl.BlockSpec((2, LEN, LEN), lambda s, g: (s * PAIRS + g, 0, 0))
BIAS = pl.BlockSpec((1, 2, LEN), lambda s, g: (g, 0, 0))
SHIFT = pl.BlockSpec((1, 2, LEN), lambda s, g: (s * PAIRS + g, 0, 0))


def cost(flops, moved):
    return pl.CostEstimate(flops=flops, bytes_accessed=moved, transcendentals=0)


def attention_fwd(queries, query_at, keys, key_at, values, value_at, bias):
    tokens = queries.shape[0]
    sequences = tokens // LEN
    specs = [lane_block(query_at), lane_block(key_at), lane_block(value_at)]
    operands = [queries, keys, values]
    if bias is not None:
        specs.append(BIAS)
        operands.append(bias)
    return pl.pallas_call(
        cross_fwd_kernel if bias is None else self_fwd_kernel,
        grid=(sequences, PAIRS),
        in_specs=specs,
        out_specs=[lane_block(0), PROBS],
        out_shape=[
            jax.ShapeDtypeStruct((tokens, HALF), bf16),
            jax.ShapeDtypeStruct((sequences * PAIRS * 2, LEN, LEN), bf16),
        ],
        cost_estimate=cost(4 * tokens * LEN * HALF * 4, tokens * LEN * 12),
    )(*operands)


def attention_bwd(queries, query_at, keys, key_at, values, value_at, grads, probs, causal):
    tokens = queries.shape[0]
    sequences = tokens // LEN
    piece = jax.ShapeDtypeStruct((tokens, HALF), bf16)
    out_shape = [piece] * 3
    out_specs = [lane_block(0)] * 3
    if causal:
        out_shape.append(jax.ShapeDtypeStruct((sequences * PAIRS, 2, LEN), f32))
        out_specs.append(SHIFT)
    return pl.pallas_call(
        self_bwd_kernel if causal else cross_bwd_kernel,
        grid=(sequences, PAIRS),
        in_specs=[lane_block(query_at), lane_block(key_at), lane_block(value_at), lane_block(0), PROBS],
        out_specs=out_specs,
        out_shape=out_shape,
        scratch_shapes=[pltpu.VMEM((LEN, LEN), bf16)],
        cost_estimate=cost(8 * tokens * LEN * HALF * 4, tokens * LEN * 12),
    )(queries, keys, values, grads, probs)


def normalize(values, gain):
    rescale = lax.rsqrt(jnp.mean(values * values, axis=1, keepdims=True) + epsilon)
    return (values * rescale * gain).astype(bf16), rescale


def normalize_back(values, gain, rescale, grad):
    weighted = gain * grad
    inner = jnp.sum(values * weighted, axis=1, keepdims=True)
    input_grad = rescale * weighted - values * (rescale * rescale * rescale) / D * inner
    gain_grad = jnp.sum(grad * values * rescale, axis=0, keepdims=True)
    return input_grad, gain_grad


def gelu_parts(v):
    root = 0.7978845608028654
    cubic = 0.044715
    bent = jnp.tanh(root * (v + cubic * (v * v * v)))
    value = 0.5 * v * (1.0 + bent)
    slope = 0.5 * (1.0 + bent) + 0.5 * v * (1.0 - bent * bent) * root * (1.0 + 3.0 * cubic * v * v)
    return value, slope


def sum_over_dp(block, dp_count):
    index = lax.axis_index("dp")
    undo = []
    bit = 1
    while bit < dp_count:
        pairs = [(i, i ^ bit) for i in range(dp_count)]
        rows = block.shape[0]
        side = lax.bitwise_and(lax.div(index, jnp.int32(bit)), jnp.int32(1))
        if rows % 32 == 0:
            low, high = block[: rows // 2], block[rows // 2 :]
            keep = jnp.where(side == 0, low, high)
            send = jnp.where(side == 0, high, low)
            block = (keep.astype(f32) + lax.ppermute(send, "dp", pairs).astype(f32)).astype(bf16)
            undo.append((side, pairs))
        else:
            block = (block.astype(f32) + lax.ppermute(block, "dp", pairs).astype(f32)).astype(bf16)
        bit *= 2
    for side, pairs in reversed(undo):
        other = lax.ppermute(block, "dp", pairs)
        block = jnp.where(
            side == 0,
            jnp.concatenate([block, other], axis=0),
            jnp.concatenate([other, block], axis=0),
        )
    return block


def reduce_group(pieces, dp_count):
    summed = []
    for own, other in pieces:
        arrived = over_col(other)
        summed.append((own.astype(f32) + arrived.astype(f32)).astype(bf16))
    whole = jnp.concatenate(summed, axis=1)
    arrived = over_row(whole[HALF:])
    block = (whole[:HALF].astype(f32) + arrived.astype(f32)).astype(bf16)
    return sum_over_dp(block, dp_count).astype(f32)


def local(
    layer_input,
    encoder_states,
    cotangent,
    buckets,
    gain_self,
    gain_cross,
    gain_ffn,
    self_query,
    self_key,
    self_value,
    self_out,
    cross_query,
    cross_key,
    cross_value,
    cross_out,
    ffn_gate,
    ffn_up,
    ffn_down,
    rel_table,
    dp_count,
):
    r = lax.axis_index("row")
    c = lax.axis_index("col")
    own_small = jnp.concatenate([gain_self, gain_cross, gain_ffn, rel_table.reshape(-1)])
    small = lax.all_gather(own_small, ("row", "col"), axis=0, tiled=False)
    quarter = gain_self.shape[0]
    gains = [
        local_order(small[:, i * quarter : (i + 1) * quarter].reshape(1, D), r, 1) for i in range(3)
    ]
    tables = small[:, 3 * quarter :].reshape(2, 2, 3, NB).transpose(1, 0, 2, 3)
    tables = local_order(tables.reshape(2, 2 * 3, NB), c, 0)
    onehot = (buckets[:, None] == jnp.arange(NB, dtype=jnp.int32)[None, :]).astype(f32)
    placed = jnp.roll(onehot[::-1], LEN - BLK + 1, axis=0)
    bias_rows = lax.dot_general(
        tables.reshape(12, NB), placed, (((1,), (1,)), ((), ())), precision=lax.Precision.HIGHEST
    ).reshape(2, PAIRS, 2, LEN)

    def columns_weight(own):
        mine = jnp.concatenate([own, over_row(own)], axis=0)
        return mine, over_col(mine)

    def rows_weight(own):
        mine = jnp.concatenate([own, over_row(own)], axis=1)
        return mine, over_col(mine)

    self_w = columns_weight(jnp.concatenate([self_query, self_key, self_value], axis=1))
    self_o = rows_weight(self_out)
    cross_kv_w = columns_weight(jnp.concatenate([cross_key, cross_value], axis=1))
    cross_q_w = columns_weight(cross_query)
    cross_o = rows_weight(cross_out)
    ffn_w = columns_weight(jnp.concatenate([ffn_gate, ffn_up], axis=1))
    ffn_d = rows_weight(ffn_down)

    x = local_order(layer_input, r, 1).astype(f32)
    encoder = local_order(encoder_states, r, 1)
    out_grad = local_order(cotangent, r, 1)
    both = range(2)

    normed_one, rescale_one = normalize(x, gains[0])
    qkv = [dot(normed_one, self_w[h]).astype(bf16) for h in both]
    self_att = [
        attention_fwd(qkv[h], 0, qkv[h], PAIRS, qkv[h], 2 * PAIRS, bias_rows[h]) for h in both
    ]
    middle = x + dot(self_att[0][0], self_o[0]) + dot(self_att[1][0], self_o[1])
    normed_two, rescale_two = normalize(middle, gains[1])
    kv = [dot(encoder, cross_kv_w[h]).astype(bf16) for h in both]
    cq = [dot(normed_two, cross_q_w[h]).astype(bf16) for h in both]
    cross_att = [attention_fwd(cq[h], 0, kv[h], 0, kv[h], PAIRS, None) for h in both]
    after = middle + dot(cross_att[0][0], cross_o[0]) + dot(cross_att[1][0], cross_o[1])
    normed_three, rescale_three = normalize(after, gains[2])
    wide = ffn_gate.shape[1]
    gate_up = [dot(normed_three, ffn_w[h]) for h in both]
    parts = [gelu_parts(gate_up[h][:, :wide]) for h in both]
    hidden = [(parts[h][0] * gate_up[h][:, wide:]).astype(bf16) for h in both]
    layer_output = after + dot(hidden[0], ffn_d[0]) + dot(hidden[1], ffn_d[1])

    out_low = out_grad.astype(bf16)
    down_grads = [t_dot(out_low, hidden[h]).astype(bf16) for h in both]
    hidden_grad = [dot_t(out_low, ffn_d[h]) for h in both]
    gate_up_grad = [
        jnp.concatenate(
            [
                (hidden_grad[h] * gate_up[h][:, wide:] * parts[h][1]).astype(bf16),
                (hidden_grad[h] * parts[h][0]).astype(bf16),
            ],
            axis=1,
        )
        for h in both
    ]
    gate_up_w_grads = [t_dot(normed_three, gate_up_grad[h]).astype(bf16) for h in both]
    ffn_sum = reduce_group([gate_up_w_grads, down_grads], dp_count)
    normed_three_grad = dot_t(gate_up_grad[0], ffn_w[0]) + dot_t(gate_up_grad[1], ffn_w[1])
    third, gain_ffn_grad = normalize_back(after, gains[2], rescale_three, normed_three_grad)
    after_grad = out_grad + third

    after_low = after_grad.astype(bf16)
    cross_out_grads = [t_dot(after_low, cross_att[h][0]).astype(bf16) for h in both]
    cross_mixed = [dot_t(after_low, cross_o[h]).astype(bf16) for h in both]
    cross_back = [
        attention_bwd(cq[h], 0, kv[h], 0, kv[h], PAIRS, cross_mixed[h], cross_att[h][1], False)
        for h in both
    ]
    kv_grad = [jnp.concatenate(cross_back[h][1:3], axis=1) for h in both]
    cross_q_grads = [t_dot(normed_two, cross_back[h][0]).astype(bf16) for h in both]
    cross_kv_grads = [t_dot(encoder, kv_grad[h]).astype(bf16) for h in both]
    cross_sum = reduce_group([cross_kv_grads, cross_q_grads, cross_out_grads], dp_count)
    normed_two_grad = dot_t(cross_back[0][0], cross_q_w[0]) + dot_t(cross_back[1][0], cross_q_w[1])
    second, gain_cross_grad = normalize_back(middle, gains[1], rescale_two, normed_two_grad)
    middle_grad = after_grad + second

    middle_low = middle_grad.astype(bf16)
    self_out_grads = [t_dot(middle_low, self_att[h][0]).astype(bf16) for h in both]
    self_mixed = [dot_t(middle_low, self_o[h]).astype(bf16) for h in both]
    self_back = [
        attention_bwd(
            qkv[h], 0, qkv[h], PAIRS, qkv[h], 2 * PAIRS, self_mixed[h], self_att[h][1], True
        )
        for h in both
    ]
    qkv_grad = [jnp.concatenate(self_back[h][:3], axis=1) for h in both]
    self_w_grads = [t_dot(normed_one, qkv_grad[h]).astype(bf16) for h in both]
    self_sum = reduce_group([self_w_grads, self_out_grads], dp_count)
    normed_one_grad = dot_t(qkv_grad[0], self_w[0]) + dot_t(qkv_grad[1], self_w[1])
    first, gain_self_grad = normalize_back(x, gains[0], rescale_one, normed_one_grad)
    input_grad = middle_grad + first

    encoder_grad = dot_t(kv_grad[0], cross_kv_w[0]) + dot_t(kv_grad[1], cross_kv_w[1])

    shift_sums = jnp.stack(
        [jnp.sum(self_back[h][3].reshape(-1, PAIRS * 2, LEN), axis=0) for h in both], axis=0
    )
    table_local = jnp.dot(
        shift_sums.reshape(12, LEN), placed, precision=lax.Precision.HIGHEST
    ).reshape(2, 2, 3, NB)
    table_all = local_order(table_local, c, 0)
    gains_all = local_order(
        jnp.concatenate([gain_self_grad, gain_cross_grad, gain_ffn_grad], axis=0), r, 1
    )
    small_all = lax.psum(
        jnp.concatenate([gains_all.reshape(-1), table_all.reshape(-1)]), ("dp", "row", "col")
    )
    gains_sum = small_all[: 3 * D].reshape(3, D)
    table_sum = small_all[3 * D :].reshape(2, 2, 3, NB)
    start = (r * 2 + c) * quarter
    gains_own = lax.dynamic_slice_in_dim(gains_sum, start, quarter, 1)
    table_own = lax.dynamic_slice(table_sum, (c, r, 0, 0), (1, 1, 3, NB))

    hw = self_query.shape[1]
    back_order = lambda v: local_order(v, r, 1)
    return (
        back_order(layer_output),
        back_order(input_grad),
        back_order(encoder_grad),
        gains_own[0],
        gains_own[1],
        gains_own[2],
        self_sum[:, :hw],
        self_sum[:, hw : 2 * hw],
        self_sum[:, 2 * hw : 3 * hw],
        self_sum[:, 3 * hw :].T,
        cross_sum[:, 2 * hw : 3 * hw],
        cross_sum[:, :hw],
        cross_sum[:, hw : 2 * hw],
        cross_sum[:, 3 * hw :].T,
        ffn_sum[:, :wide],
        ffn_sum[:, wide : 2 * wide],
        ffn_sum[:, 2 * wide :].T,
        table_own,
    )


def solution(mesh):
    tokens = P(("dp", "row", "col"), None)
    gain = P(("row", "col"))
    columns = P("row", "col")
    rows = P("col", "row")
    table = P("col", "row", None, None)
    weights = (columns,) * 3 + (rows,) + (columns,) * 3 + (rows,) + (columns,) * 2 + (rows,)
    in_specs = (tokens,) * 3 + (P(),) + (gain,) * 3 + weights + (table,)
    out_specs = (tokens,) * 3 + (gain,) * 3 + weights + (table,)
    body = functools.partial(local, dp_count=mesh.shape["dp"])
    return jax.shard_map(
        body, mesh=mesh, in_specs=in_specs, out_specs=out_specs, check_vma=False
    )
```

time: 4440 us -> 633 us (0.14)
  blocking collectives: 2300 us -> 119 us
  local copies, waits for them, and re-layouts: 910 us -> 48.2 us
  waiting for transfers between devices: 798 us -> 176 us
  matrix products: 224 us -> 118 us
  Pallas kernels: 0 us -> 90.2 us
  other arithmetic: 116 us -> 30.3 us
    unnamed x5 -> x1, blocking collectives: 2190 us -> 57 us
    reduce_scatter x4 -> x0, waiting for transfers between devices: 446 us -> none  [reduce_rows(): lax.psum_scatter(partial_value, 'row', scatter_dimension=2, tiled=True)]
    all_gather x14 -> x0, waiting for transfers between devices: 245 us -> none  [the longest x7 210 us: gather_rows(): lax.all_gather(as_sent(operand), 'row', axis=2, tiled=True)]
    ppermute x0 -> x42, waiting for transfers between devices: none -> 176 us  [the longest x10 74.2 us: over_row(): return lax.ppermute(x, 'row', SWAP)]
    another operation x51 -> x0, local copies, waits for them, and re-layouts: 175 us -> none  [the longest x16 135 us: block_bias(): jnp.tile(shifted, (1, block_rows))[:, :block_rows * (shift_count - 1)]]
    reshape x22 -> x15, local copies, waits for them, and re-layouts: 155 us -> 2.31 us  [the longest x2 1.44 us: local(): self_back[h][3].reshape(-1, PAIRS * 2, LEN)]
    slice x30 -> x8, local copies, waits for them, and re-layouts: 116 us -> 2.05 us  [the longest x1 1.09 us: reduce_group(): arrived = over_row(whole[HALF:])]
    dot_general x82 -> x44, matrix products: 224 us -> 118 us  [the longest x14 47.5 us: dot_t(): lax.dot_general(a, b, (((1,), (1,)), ((), ())), preferred_element_type=f32)]
  transfers between devices with their start and end apart: 26 -> 42, of which waited for: 19 -> 14; matrix products, arithmetic and copies ran while one was open for 15% -> 18% of each run, Pallas kernels for 0% -> 7%
where the time goes in v1:
time: 633 us; the launch traced here: 628 us
  waiting for transfers between devices  176 us (28%)
  blocking collectives  119 us (19%)
  matrix products  118 us (19%)
  Pallas kernels  90.2 us (14%)
  local copies, waits for them, and re-layouts  48.2 us (8%)
  starting transfers between devices  43.8 us (7%)
  other arithmetic  30.3 us (5%)
    ppermute x10, waiting for transfers between devices, over_row(): return lax.ppermute(x, 'row', SWAP)  74.2 us
    psum x1, blocking collectives, local(): lax.psum(jnp.concatenate([gains_all.reshape(-1), table_all.reshape(-1)]),...  62.1 us
    unnamed x1, blocking collectives  57 us
    ppermute x9, waiting for transfers between devices, sum_over_dp(): lax.ppermute(send, 'dp', pairs).astype(f32)  53.5 us
    ppermute x9, waiting for transfers between devices, sum_over_dp(): other = lax.ppermute(block, 'dp', pairs)  48.1 us
    dot_general x14, matrix products, dot_t(): lax.dot_general(a, b, (((1,), (1,)), ((), ())), preferred_element_type=f32)  47.5 us
    pallas_call x4, Pallas kernels, attention_bwd(): pl.pallas_call(self_bwd_kernel if causal else cross_bwd_kernel, grid=(seq...  47.1 us
    pallas_call x4, Pallas kernels, attention_fwd(): pl.pallas_call(cross_fwd_kernel if bias is None else self_fwd_kernel, gri...  43.2 us
  transfers between devices with their start and end apart: 42, of which 14 were waited for; matrix products, arithmetic and copies ran while one was open for 18% of the time, Pallas kernels for 7%

profile of v1, /device:TPU:0, one launch (start us, length us, event | category | flops | bytes accessed | tf_op | source)
XLA Modules:
  0.0 628.3 jit_solution(567430638731614289)
XLA Ops:
  3.9 3.0 collective-permute-start
  12.5 57.0 %all-reduce = f32[2688]{0:T(1024)S(1)} all-reduce(f32[2688]{0:T(1024)S(1)} %maximum_dynamic-update-slice_fusion), channel_id=2, replica_groups=mesh['dp'=8,'row'=2,'col'=2] {'row','col'}, use_global_device_ids=true, to_apply=%add | all-reduce | flops 2688 | bytes 21504
  72.1 2.1 constant_dynamic-update-slice_fusion.14
  77.8 2.2 constant_dynamic-update-slice_fusion.12
  95.9 2.6 pad_maximum_fusion.5
  98.5 6.0 collective-permute-done.5
  107.8 2.1 constant_dynamic-update-slice_fusion.13
  109.9 3.4 convolution_convert_fusion.5.q_ref.k_ref.v_ref
  113.3 10.2 %shard_map.322 = (bf16[512,384]{1,0:T(8,128)(2,1)}, bf16[6,512,512]{2,1,0:T(8,128)(2,1)}) custom-call(bf16[512,1152]{1,0:T(8,128)(2,1)} %convolution_convert_fusion.5.q_ref.k_ref.v_ref, bf16[512,1152]{1,0:T(8,128)(2,1)} %convolution_convert_fusion.5.q_ref.k_ref.v_ref, bf16[512,1152]{1,0:T(8,128)(2,1)} %convolution_convert_fusion.5.q_ref.k_ref.v_ref, ...), custom_call_target="tpu_custom_call" | custom-call | flops 1610612736 | bytes 3145728 | tf_op jit(solution)/shard_map/pallas_call | solution.py:171
  123.5 2.8 fusion.69
  126.3 9.2 %collective-permute-done.10 = bf16[384,2048]{1,0:T(8,128)(2,1)} collective-permute-done((bf16[384,2048]{1,0:T(8,128)(2,1)}, bf16[384,2048]{1,0:T(8,128)(2,1)}, u32[]{:S(2)}, u32[]{:S(2)}) %collective-permute-start.10) | collective-permute-done | bytes 1572896 | tf_op jit(solution)/shard_map/ppermute | solution.py:26
  135.5 3.9 pad_maximum_fusion
  139.9 2.9 convolution_convert_fusion.10.k_ref.v_ref
  142.9 3.7 convolution_convert_fusion.4.q_ref.k_ref.v_ref
  146.6 10.3 %shard_map.323 = (bf16[512,384]{1,0:T(8,128)(2,1)}, bf16[6,512,512]{2,1,0:T(8,128)(2,1)}) custom-call(bf16[512,1152]{1,0:T(8,128)(2,1)} %convolution_convert_fusion.4.q_ref.k_ref.v_ref, bf16[512,1152]{1,0:T(8,128)(2,1)} %convolution_convert_fusion.4.q_ref.k_ref.v_ref, bf16[512,1152]{1,0:T(8,128)(2,1)} %convolution_convert_fusion.4.q_ref.k_ref.v_ref, ...), custom_call_target="tpu_custom_call" | custom-call | flops 1610612736 | bytes 3145728 | tf_op jit(solution)/shard_map/pallas_call | solution.py:171
  157.0 2.4 multiply_reduce_fusion.5
  161.8 2.4 convolution_convert_fusion.22.q_ref
  164.2 11.3 %shard_map.324 = (bf16[512,384]{1,0:T(8,128)(2,1)}, bf16[6,512,512]{2,1,0:T(8,128)(2,1)}) custom-call(bf16[512,384]{1,0:T(8,128)(2,1)} %convolution_convert_fusion.23.q_ref, bf16[512,768]{1,0:T(8,128)(2,1)} %convolution_convert_fusion.11.k_ref.v_ref, bf16[512,768]{1,0:T(8,128)(2,1)} %convolution_convert_fusion.11.k_ref.v_ref), custom_call_target="tpu_custom_call" | custom-call | flops 1610612736 | bytes 3145728 | tf_op jit(solution)/shard_map/pallas_call | solution.py:171
  175.4 11.4 %shard_map.325 = (bf16[512,384]{1,0:T(8,128)(2,1)}, bf16[6,512,512]{2,1,0:T(8,128)(2,1)}) custom-call(bf16[512,384]{1,0:T(8,128)(2,1)} %convolution_convert_fusion.22.q_ref, bf16[512,768]{1,0:T(8,128)(2,1)} %convolution_convert_fusion.10.k_ref.v_ref, bf16[512,768]{1,0:T(8,128)(2,1)} %convolution_convert_fusion.10.k_ref.v_ref), custom_call_target="tpu_custom_call" | custom-call | flops 1610612736 | bytes 3145728 | tf_op jit(solution)/shard_map/pallas_call | solution.py:171
  189.8 4.0 fusion.53
  193.8 3.8 fusion.14
  197.6 3.5 fusion.71
  201.2 3.7 fusion.72
  204.9 15.2 %fusion.19 = (bf16[512,1024]{1,0:T(8,128)(2,1)S(1)}, bf16[512,1024]{1,0:T(8,128)(2,1)S(1)}, bf16[512,1024]{1,0:T(8,128)(2,1)S(1)}) fusion(f32[512,2048]{1,0:T(8,128)S(1)} %fusion.72, bf16[512,768]{1,0:T(8,128)(2,1)S(1)} %copy-done.42, bf16[1024,768]{1,0:T(8,128)(2,1)} %collective-permute-done.13), kind=kOutput, calls=%fused_computation.51 | convolution fusion | flops 818413568 | bytes 9699328 | tf_op jit(solution)/shard_map/dot_general | solution.py:38
  220.1 4.8 fusion.30
  225.0 4.2 multiply_reduce_fusion
  229.2 3.9 fusion.55
  234.7 2.4 convolution_convert_fusion.20.g_ref
  237.1 11.9 %shard_map.327 = (bf16[512,384]{1,0:T(8,128)(2,1)}, bf16[512,384]{1,0:T(8,128)(2,1)}, bf16[512,384]{1,0:T(8,128)(2,1)}) custom-call(bf16[512,384]{1,0:T(8,128)(2,1)} %convolution_convert_fusion.22.q_ref, bf16[512,768]{1,0:T(8,128)(2,1)} %convolution_convert_fusion.10.k_ref.v_ref, bf16[512,768]{1,0:T(8,128)(2,1)} %convolution_convert_fusion.10.k_ref.v_ref, ...), custom_call_target="tpu_custom_call" | custom-call | flops 3221225472 | bytes 3145728 | tf_op jit(solution)/shard_map/pallas_call | solution.py:193
  249.0 11.9 %shard_map.326 = (bf16[512,384]{1,0:T(8,128)(2,1)}, bf16[512,384]{1,0:T(8,128)(2,1)}, bf16[512,384]{1,0:T(8,128)(2,1)}) custom-call(bf16[512,384]{1,0:T(8,128)(2,1)} %convolution_convert_fusion.23.q_ref, bf16[512,768]{1,0:T(8,128)(2,1)} %convolution_convert_fusion.11.k_ref.v_ref, bf16[512,768]{1,0:T(8,128)(2,1)} %convolution_convert_fusion.11.k_ref.v_ref, ...), custom_call_target="tpu_custom_call" | custom-call | flops 3221225472 | bytes 3145728 | tf_op jit(solution)/shard_map/pallas_call | solution.py:193
  267.1 2.4 convolution_convert_fusion.18.g_ref
  269.5 11.4 %shard_map.329 = (bf16[512,384]{1,0:T(8,128)(2,1)}, bf16[512,384]{1,0:T(8,128)(2,1)}, bf16[512,384]{1,0:T(8,128)(2,1)}, f32[3,2,512]{2,1,0:T(2,128)}) custom-call(bf16[512,1152]{1,0:T(8,128)(2,1)} %convolution_convert_fusion.4.q_ref.k_ref.v_ref, bf16[512,1152]{1,0:T(8,128)(2,1)} %convolution_convert_fusion.4.q_ref.k_ref.v_ref, ...), custom_call_target="tpu_custom_call" | custom-call | flops 3221225472 | bytes 3145728 | tf_op jit(solution)/shard_map/pallas_call | solution.py:193
  281.7 11.9 %shard_map.328 = (bf16[512,384]{1,0:T(8,128)(2,1)}, bf16[512,384]{1,0:T(8,128)(2,1)}, bf16[512,384]{1,0:T(8,128)(2,1)}, f32[3,2,512]{2,1,0:T(2,128)}) custom-call(bf16[512,1152]{1,0:T(8,128)(2,1)} %convolution_convert_fusion.5.q_ref.k_ref.v_ref, bf16[512,1152]{1,0:T(8,128)(2,1)} %convolution_convert_fusion.5.q_ref.k_ref.v_ref, ...), custom_call_target="tpu_custom_call" | custom-call | flops 3221225472 | bytes 3145728 | tf_op jit(solution)/shard_map/pallas_call | solution.py:193
  294.7 2.5 convolution_convert_fusion.16
  297.2 2.8 convolution_convert_fusion.12
  301.4 2.2 convolution_convert_fusion.6
  303.6 3.5 convolution_convert_fusion
  309.7 2.5 convolution_convert_fusion.2
  312.4 3.1 fusion.74
  315.6 2.8 fusion.29
  323.4 2.4 fusion.75
  329.1 3.2 maximum_select_fusion.1
  332.8 2.8 maximum_select_fusion.3
  338.9 2.1 add_convert_fusion.6
  345.0 62.1 %psum.7 = f32[2688]{0:T(1024)S(1)} all-reduce(f32[2688]{0:T(1024)S(1)} %pad_maximum_fusion.17), channel_id=1, replica_groups=mesh['dp'=8,'row'=2,'col'=2] {'dp','row','col'}, use_global_device_ids=true, to_apply=%region_9.10 | all-reduce | flops 2688 | bytes 21504 | tf_op jit(solution)/shard_map/psum | solution.py:403
  410.9 2.6 add_convert_fusion.3
  415.3 2.3 collective-permute-start.27
  417.6 2.8 add_convert_fusion.2
  421.6 8.0 %collective-permute-done.27 = bf16[192,1536]{1,0:T(8,128)(2,1)S(1)} collective-permute-done((bf16[192,1536]{1,0:T(8,128)(2,1)S(1)}, bf16[192,1536]{1,0:T(8,128)(2,1)S(1)}, u32[]{:S(2)}, u32[]{:S(2)}) %collective-permute-start.27) | collective-permute-done | bytes 589856 | tf_op jit(solution)/shard_map/ppermute | solution.py:238
  429.9 3.8 add_convert_fusion
  435.8 13.7 %collective-permute-done.16 = bf16[384,1536]{1,0:T(8,128)(2,1)S(1)} collective-permute-done((bf16[384,1536]{1,0:T(8,128)(2,1)S(1)}, bf16[384,1536]{1,0:T(8,128)(2,1)S(1)}, u32[]{:S(2)}, u32[]{:S(2)}) %collective-permute-start.16) | collective-permute-done | bytes 1179680 | tf_op jit(solution)/shard_map/ppermute | solution.py:26
  451.7 45.2 %collective-permute-done.35 = bf16[384,3072]{1,0:T(8,128)(2,1)S(1)} collective-permute-done((bf16[384,3072]{1,0:T(8,128)(2,1)S(1)}, bf16[384,3072]{1,0:T(8,128)(2,1)S(1)}, u32[]{:S(2)}, u32[]{:S(2)}) %collective-permute-start.35) | collective-permute-done | bytes 2359328 | tf_op jit(solution)/shard_map/ppermute | solution.py:26
  501.8 21.0 %collective-permute-done.36 = bf16[192,3072]{1,0:T(8,128)(2,1)S(1)} collective-permute-done((bf16[192,3072]{1,0:T(8,128)(2,1)S(1)}, bf16[192,3072]{1,0:T(8,128)(2,1)S(1)}, u32[]{:S(2)}, u32[]{:S(2)}) %collective-permute-start.36) | collective-permute-done | bytes 1179680 | tf_op jit(solution)/shard_map/ppermute | solution.py:238
  525.8 12.0 %collective-permute-done.37 = bf16[96,3072]{1,0:T(8,128)(2,1)S(1)} collective-permute-done((bf16[96,3072]{1,0:T(8,128)(2,1)S(1)}, bf16[96,3072]{1,0:T(8,128)(2,1)S(1)}, u32[]{:S(2)}, u32[]{:S(2)}) %collective-permute-start.37) | collective-permute-done | bytes 589856 | tf_op jit(solution)/shard_map/ppermute | solution.py:238
  538.3 3.0 collective-permute-start.20
  541.2 12.5 %collective-permute-done.38 = bf16[48,3072]{1,0:T(8,128)(2,1)S(1)} collective-permute-done((bf16[48,3072]{1,0:T(8,128)(2,1)S(1)}, bf16[48,3072]{1,0:T(8,128)(2,1)S(1)}, u32[]{:S(2)}, u32[]{:S(2)}) %collective-permute-start.38) | collective-permute-done | bytes 294944 | tf_op jit(solution)/shard_map/ppermute | solution.py:238
  554.0 2.9 collective-permute-start.31
  556.9 5.4 collective-permute-start.21
  562.3 7.4 %collective-permute-done.39 = bf16[48,3072]{1,0:T(8,128)(2,1)S(1)} collective-permute-done((bf16[48,3072]{1,0:T(8,128)(2,1)S(1)}, bf16[48,3072]{1,0:T(8,128)(2,1)S(1)}, u32[]{:S(2)}, u32[]{:S(2)}) %collective-permute-start.39) | collective-permute-done | bytes 294944 | tf_op jit(solution)/shard_map/ppermute | solution.py:244
  572.9 4.3 collective-permute-done.21
  579.2 9.7 %collective-permute-done.40 = bf16[96,3072]{1,0:T(8,128)(2,1)S(1)} collective-permute-done((bf16[96,3072]{1,0:T(8,128)(2,1)S(1)}, bf16[96,3072]{1,0:T(8,128)(2,1)S(1)}, u32[]{:S(2)}, u32[]{:S(2)}) %collective-permute-start.40) | collective-permute-done | bytes 589856 | tf_op jit(solution)/shard_map/ppermute | solution.py:244
  593.7 6.4 %collective-permute-done.22 = bf16[192,1536]{1,0:T(8,128)(2,1)} collective-permute-done((bf16[192,1536]{1,0:T(8,128)(2,1)S(1)}, bf16[192,1536]{1,0:T(8,128)(2,1)}, u32[]{:S(2)}, u32[]{:S(2)}) %collective-permute-start.22) | collective-permute-done | bytes 589856 | tf_op jit(solution)/shard_map/ppermute | solution.py:244
  604.0 19.8 %collective-permute-done.41 = bf16[192,3072]{1,0:T(8,128)(2,1)S(1)} collective-permute-done((bf16[192,3072]{1,0:T(8,128)(2,1)S(1)}, bf16[192,3072]{1,0:T(8,128)(2,1)S(1)}, u32[]{:S(2)}, u32[]{:S(2)}) %collective-permute-start.41) | collective-permute-done | bytes 1179680 | tf_op jit(solution)/shard_map/ppermute | solution.py:244
  624.5 2.0 slice_bitcast_fusion
  (406 shorter events, 104.7 us)
Async XLA Ops:
  0.7 10.4 %copy-start.79 = (u32[32]{0:T(128)S(1)}, u32[32]{0:T(128)}, u32[]{:S(2)}) copy-start(u32[32]{0:T(128)} %constant.53) | copy-start | bytes 388
  0.7 10.3 %copy-start.75 = (f32[1,1,3,32]{3,1,2,0:T(1,128)S(1)}, f32[1,1,3,32]{3,1,2,0:T(1,128)}, u32[]{:S(2)}) copy-start(f32[1,1,3,32]{3,1,2,0:T(1,128)} %param.37) | copy-start | bytes 1156
  0.7 11.6 %copy-start.76 = (f32[192]{0:T(256)S(1)}, f32[192]{0:T(256)}, u32[]{:S(2)}) copy-start(f32[192]{0:T(256)} %param.25) | copy-start | bytes 2308
  0.7 11.6 %copy-start.77 = (f32[192]{0:T(256)S(1)}, f32[192]{0:T(256)}, u32[]{:S(2)}) copy-start(f32[192]{0:T(256)} %param.24) | copy-start | bytes 2308
  0.7 11.6 %copy-start.78 = (f32[192]{0:T(256)S(1)}, f32[192]{0:T(256)}, u32[]{:S(2)}) copy-start(f32[192]{0:T(256)} %param.23) | copy-start | bytes 2308
  2.7 71.4 %copy-start.19 = (bf16[512,768]{1,0:T(8,128)(2,1)S(1)}, bf16[512,768]{1,0:T(8,128)(2,1)}, u32[]{:S(2)}) copy-start(bf16[512,768]{1,0:T(8,128)(2,1)} %param.19) | copy-start | bytes 2359300
  3.8 106.1 %copy-start.24 = (bf16[384,1152]{1,0:T(8,128)(2,1)}, bf16[384,1152]{1,0:T(8,128)(2,1)S(1)}, u32[]{:S(2)}) copy-start(bf16[384,1152]{1,0:T(8,128)(2,1)S(1)} %constant_dynamic-update-slice_fusion) | copy-start | bytes 2654212
  3.9 91.6 %collective-permute-start = (bf16[384,1152]{1,0:T(8,128)(2,1)S(1)}, bf16[384,1152]{1,0:T(8,128)(2,1)}, u32[]{:S(2)}, u32[]{:S(2)}) collective-permute-start(bf16[384,1152]{1,0:T(8,128)(2,1)S(1)} %constant_dynamic-update-slice_fusion), channel_id=1, source_target_pairs={{0,2},{2,0},{1,3},{3,1},{4,6},{6,4},{5,7},{7,5},{8,10},{10,8},{9,1... | collective-permute-start | bytes 2654216 | tf_op jit(solution)/shard_map/ppermute | solution.py:26
  6.9 81.4 %collective-permute-start.1 = (bf16[384,384]{1,0:T(8,128)(2,1)}, bf16[384,384]{1,0:T(8,128)(2,1)}, u32[]{:S(2)}, u32[]{:S(2)}) collective-permute-start(bf16[384,384]{1,0:T(8,128)(2,1)} %param.29), channel_id=1, source_target_pairs={{0,2},{2,0},{1,3},{3,1},{4,6},{6,4},{5,7},{7,5},{8,10},{10,8},{9,1... | collective-permute-start | bytes 884744 | tf_op jit(solution)/shard_map/ppermute | solution.py:26
  7.0 83.3 %collective-permute-start.4 = (bf16[384,384]{1,0:T(8,128)(2,1)}, bf16[384,384]{1,0:T(8,128)(2,1)}, u32[]{:S(2)}, u32[]{:S(2)}) collective-permute-start(bf16[384,384]{1,0:T(8,128)(2,1)} %param.30), channel_id=1, source_target_pairs={{0,2},{2,0},{1,3},{3,1},{4,6},{6,4},{5,7},{7,5},{8,10},{10,8},{9,1... | collective-permute-start | bytes 884744 | tf_op jit(solution)/shard_map/ppermute | solution.py:26
  8.9 84.8 %collective-permute-start.6 = (bf16[384,384]{1,0:T(8,128)(2,1)}, bf16[384,384]{1,0:T(8,128)(2,1)}, u32[]{:S(2)}, u32[]{:S(2)}) collective-permute-start(bf16[384,384]{1,0:T(8,128)(2,1)} %param.33), channel_id=1, source_target_pairs={{0,2},{2,0},{1,3},{3,1},{4,6},{6,4},{5,7},{7,5},{8,10},{10,8},{9,1... | collective-permute-start | bytes 884744 | tf_op jit(solution)/shard_map/ppermute | solution.py:26
  9.0 98.4 %collective-permute-start.11 = (bf16[1024,384]{1,0:T(8,128)(2,1)}, bf16[1024,384]{1,0:T(8,128)(2,1)}, u32[]{:S(2)}, u32[]{:S(2)}) collective-permute-start(bf16[1024,384]{1,0:T(8,128)(2,1)} %param.36), channel_id=1, source_target_pairs={{0,2},{2,0},{1,3},{3,1},{4,6},{6,4},{5,7},{7,5},{8,10},{10,8},{9,1... | collective-permute-start | bytes 2359304 | tf_op jit(solution)/shard_map/ppermute | solution.py:26
  76.7 80.3 %copy-start.5 = (bf16[512,768]{1,0:T(8,128)(2,1)}, bf16[512,768]{1,0:T(8,128)(2,1)S(1)}, u32[]{:S(2)}) copy-start(bf16[512,768]{1,0:T(8,128)(2,1)S(1)} %get-tuple-element.137) | copy-start | bytes 2359300
  87.0 18.7 %copy-start.14 = (bf16[384,768]{1,0:T(8,128)(2,1)}, bf16[384,768]{1,0:T(8,128)(2,1)S(1)}, u32[]{:S(2)}) copy-start(bf16[384,768]{1,0:T(8,128)(2,1)S(1)} %constant_dynamic-update-slice_fusion.7) | copy-start | bytes 1769476
  88.3 16.3 %collective-permute-start.5 = (bf16[384,768]{1,0:T(8,128)(2,1)S(1)}, bf16[384,768]{1,0:T(8,128)(2,1)S(1)}, u32[]{:S(2)}, u32[]{:S(2)}) collective-permute-start(bf16[384,768]{1,0:T(8,128)(2,1)S(1)} %constant_dynamic-update-slice_fusion.7), channel_id=1, source_target_pairs={{0,2},{2,0},{1,3},{3,1},{4,6},{6,4},{5,7},{7,5},{8,10},{10,8},{9,1... | collective-permute-start | bytes 1769480 | tf_op jit(solution)/shard_map/ppermute | solution.py:26
  90.3 45.2 %collective-permute-start.10 = (bf16[384,2048]{1,0:T(8,128)(2,1)}, bf16[384,2048]{1,0:T(8,128)(2,1)}, u32[]{:S(2)}, u32[]{:S(2)}) collective-permute-start(bf16[384,2048]{1,0:T(8,128)(2,1)} %constant_dynamic-update-slice_fusion.11), channel_id=1, source_target_pairs={{0,2},{2,0},{1,3},{3,1},{4,6},{6,4},{5,7},{7,5},{8,10},{10,8},{9,1... | collective-permute-start | bytes 4718600 | tf_op jit(solution)/shard_map/ppermute | solution.py:26
  93.7 63.3 %collective-permute-start.3 = (bf16[384,768]{1,0:T(8,128)(2,1)}, bf16[384,768]{1,0:T(8,128)(2,1)}, u32[]{:S(2)}, u32[]{:S(2)}) collective-permute-start(bf16[384,768]{1,0:T(8,128)(2,1)} %constant_dynamic-update-slice_fusion.3), channel_id=1, source_target_pairs={{0,1},{1,0},{2,3},{3,2},{4,5},{5,4},{6,7},{7,6},{8,9},{9,8},{10,11... | collective-permute-start | bytes 1769480 | tf_op jit(solution)/shard_map/ppermute | solution.py:30
  95.4 66.3 %collective-permute-start.7 = (bf16[768,384]{1,0:T(8,128)(2,1)}, bf16[768,384]{1,0:T(8,128)(2,1)}, u32[]{:S(2)}, u32[]{:S(2)}) collective-permute-start(bf16[768,384]{1,0:T(8,128)(2,1)} %constant_dynamic-update-slice_fusion.5), channel_id=1, source_target_pairs={{0,1},{1,0},{2,3},{3,2},{4,5},{5,4},{6,7},{7,6},{8,9},{9,8},{10,11... | collective-permute-start | bytes 1769480 | tf_op jit(solution)/shard_map/ppermute | solution.py:30
  104.5 38.3 %collective-permute-start.2 = (bf16[768,1152]{1,0:T(8,128)(2,1)}, bf16[768,1152]{1,0:T(8,128)(2,1)}, u32[]{:S(2)}, u32[]{:S(2)}) collective-permute-start(bf16[768,1152]{1,0:T(8,128)(2,1)} %pad_maximum_fusion.5), channel_id=1, source_target_pairs={{0,1},{1,0},{2,3},{3,2},{4,5},{5,4},{6,7},{7,6},{8,9},{9,8},{10,11... | collective-permute-start | bytes 5308424 | tf_op jit(solution)/shard_map/ppermute | solution.py:30
  107.4 32.0 %collective-permute-start.8 = (bf16[768,768]{1,0:T(8,128)(2,1)}, bf16[768,768]{1,0:T(8,128)(2,1)}, u32[]{:S(2)}, u32[]{:S(2)}) collective-permute-start(bf16[768,768]{1,0:T(8,128)(2,1)} %pad_maximum_fusion.11), channel_id=1, source_target_pairs={{0,1},{1,0},{2,3},{3,2},{4,5},{5,4},{6,7},{7,6},{8,9},{9,8},{10,11... | collective-permute-start | bytes 3538952 | tf_op jit(solution)/shard_map/ppermute | solution.py:30
  113.3 10.2 %copy-start.28 = (bf16[384,768]{1,0:T(8,128)(2,1)S(1)}, bf16[384,768]{1,0:T(8,128)(2,1)}, u32[]{:S(2)}) copy-start(bf16[384,768]{1,0:T(8,128)(2,1)} %constant_dynamic-update-slice_fusion.3) | copy-start | bytes 1769476
  123.5 12.0 %copy-start.30 = (bf16[384,768]{1,0:T(8,128)(2,1)S(1)}, bf16[384,768]{1,0:T(8,128)(2,1)}, u32[]{:S(2)}) copy-start(bf16[384,768]{1,0:T(8,128)(2,1)} %constant_dynamic-update-slice_fusion.9) | copy-start | bytes 1769476
  126.3 13.6 %copy-start.35 = (bf16[512,768]{1,0:T(8,128)(2,1)S(1)}, bf16[512,768]{1,0:T(8,128)(2,1)}, u32[]{:S(2)}) copy-start(bf16[512,768]{1,0:T(8,128)(2,1)} %maximum_select_fusion.9) | copy-start | bytes 2359300
  135.5 51.9 %collective-permute-start.9 = (bf16[384,768]{1,0:T(8,128)(2,1)S(1)}, bf16[384,768]{1,0:T(8,128)(2,1)}, u32[]{:S(2)}, u32[]{:S(2)}) collective-permute-start(bf16[384,768]{1,0:T(8,128)(2,1)S(1)} %copy-done.30), channel_id=1, source_target_pairs={{0,1},{1,0},{2,3},{3,2},{4,5},{5,4},{6,7},{7,6},{8,9},{9,8},{10,11... | collective-permute-start | bytes 1769480 | tf_op jit(solution)/shard_map/ppermute | solution.py:30
  139.4 65.5 %collective-permute-start.13 = (bf16[1024,768]{1,0:T(8,128)(2,1)}, bf16[1024,768]{1,0:T(8,128)(2,1)}, u32[]{:S(2)}, u32[]{:S(2)}) collective-permute-start(bf16[1024,768]{1,0:T(8,128)(2,1)} %constant_dynamic-update-slice_fusion.13), channel_id=1, source_target_pairs={{0,1},{1,0},{2,3},{3,2},{4,5},{5,4},{6,7},{7,6},{8,9},{9,8},{10,11... | collective-permute-start | bytes 4718600 | tf_op jit(solution)/shard_map/ppermute | solution.py:30
  142.9 58.3 %collective-permute-start.12 = (bf16[768,2048]{1,0:T(8,128)(2,1)}, bf16[768,2048]{1,0:T(8,128)(2,1)}, u32[]{:S(2)}, u32[]{:S(2)}) collective-permute-start(bf16[768,2048]{1,0:T(8,128)(2,1)} %pad_maximum_fusion), channel_id=1, source_target_pairs={{0,1},{1,0},{2,3},{3,2},{4,5},{5,4},{6,7},{7,6},{8,9},{9,8},{10,11... | collective-permute-start | bytes 9437192 | tf_op jit(solution)/shard_map/ppermute | solution.py:30
  175.4 11.4 %copy-start.54 = (bf16[512,384]{1,0:T(8,128)(2,1)S(1)}, bf16[512,384]{1,0:T(8,128)(2,1)}, u32[]{:S(2)}) copy-start(bf16[512,384]{1,0:T(8,128)(2,1)} %get-tuple-element.42) | copy-start | bytes 1179652
  189.8 11.4 %copy-start.45 = (bf16[512,768]{1,0:T(8,128)(2,1)}, bf16[512,768]{1,0:T(8,128)(2,1)S(1)}, u32[]{:S(2)}) copy-start(bf16[512,768]{1,0:T(8,128)(2,1)S(1)} %multiply_convert_fusion.4) | copy-start | bytes 2359300
  197.6 27.4 %copy-start.82 = (bf16[512,1024]{1,0:T(8,128)(2,1)}, bf16[512,1024]{1,0:T(8,128)(2,1)S(1)}, u32[]{:S(2)}) copy-start(bf16[512,1024]{1,0:T(8,128)(2,1)S(1)} %get-tuple-element.138) | copy-start | bytes 3145732
  197.6 27.4 %copy-start.84 = (bf16[512,1024]{1,0:T(8,128)(2,1)}, bf16[512,1024]{1,0:T(8,128)(2,1)S(1)}, u32[]{:S(2)}) copy-start(bf16[512,1024]{1,0:T(8,128)(2,1)S(1)} %get-tuple-element.139) | copy-start | bytes 3145732
  233.2 73.9 %copy-start = (f32[512,768]{1,0:T(8,128)}, f32[512,768]{1,0:T(8,128)S(1)}, u32[]{:S(2)}) copy-start(f32[512,768]{1,0:T(8,128)S(1)} %get-tuple-element.159) | copy-start | bytes 4718596
  281.7 13.0 %copy-start.39 = (bf16[512,768]{1,0:T(8,128)(2,1)S(1)}, bf16[512,768]{1,0:T(8,128)(2,1)}, u32[]{:S(2)}) copy-start(bf16[512,768]{1,0:T(8,128)(2,1)} %copy-done.38) | copy-start | bytes 2359300
  328.0 81.2 %collective-permute-start.15 = (bf16[768,384]{1,0:T(8,128)(2,1)}, bf16[768,384]{1,0:T(8,128)(2,1)}, u32[]{:S(2)}, u32[]{:S(2)}) collective-permute-start(bf16[768,384]{1,0:T(8,128)(2,1)} %convolution_convert_fusion.16), channel_id=1, source_target_pairs={{0,1},{1,0},{2,3},{3,2},{4,5},{5,4},{6,7},{7,6},{8,9},{9,8},{10,11... | collective-permute-start | bytes 1769480 | tf_op jit(solution)/shard_map/ppermute | solution.py:30
  328.6 89.1 %collective-permute-start.14 = (bf16[768,1152]{1,0:T(8,128)(2,1)}, bf16[768,1152]{1,0:T(8,128)(2,1)}, u32[]{:S(2)}, u32[]{:S(2)}) collective-permute-start(bf16[768,1152]{1,0:T(8,128)(2,1)} %convolution_convert_fusion.2), channel_id=1, source_target_pairs={{0,1},{1,0},{2,3},{3,2},{4,5},{5,4},{6,7},{7,6},{8,9},{9,8},{10,11... | collective-permute-start | bytes 5308424 | tf_op jit(solution)/shard_map/ppermute | solution.py:30
  328.6 7.0 %collective-permute-start.25 = (bf16[768,384]{1,0:T(8,128)(2,1)}, bf16[768,384]{1,0:T(8,128)(2,1)}, u32[]{:S(2)}, u32[]{:S(2)}) collective-permute-start(bf16[768,384]{1,0:T(8,128)(2,1)} %convolution_convert_fusion.12), channel_id=1, source_target_pairs={{0,1},{1,0},{2,3},{3,2},{4,5},{5,4},{6,7},{7,6},{8,9},{9,8},{10,11... | collective-permute-start | bytes 1769480 | tf_op jit(solution)/shard_map/ppermute | solution.py:30
  329.1 9.5 %collective-permute-start.23 = (bf16[768,768]{1,0:T(8,128)(2,1)}, bf16[768,768]{1,0:T(8,128)(2,1)}, u32[]{:S(2)}, u32[]{:S(2)}) collective-permute-start(bf16[768,768]{1,0:T(8,128)(2,1)} %convolution_convert_fusion.8), channel_id=1, source_target_pairs={{0,1},{1,0},{2,3},{3,2},{4,5},{5,4},{6,7},{7,6},{8,9},{9,8},{10,11... | collective-permute-start | bytes 3538952 | tf_op jit(solution)/shard_map/ppermute | solution.py:30
  332.4 5.2 collective-permute-start.24
  335.6 75.3 %collective-permute-start.34 = (bf16[768,1024]{1,0:T(8,128)(2,1)}, bf16[768,1024]{1,0:T(8,128)(2,1)}, u32[]{:S(2)}, u32[]{:S(2)}) collective-permute-start(bf16[768,1024]{1,0:T(8,128)(2,1)} %convolution_convert_fusion.6), channel_id=1, source_target_pairs={{0,1},{1,0},{2,3},{3,2},{4,5},{5,4},{6,7},{7,6},{8,9},{9,8},{10,11... | collective-permute-start | bytes 4718600 | tf_op jit(solution)/shard_map/ppermute | solution.py:30
  337.6 92.3 %collective-permute-start.33 = (bf16[768,2048]{1,0:T(8,128)(2,1)}, bf16[768,2048]{1,0:T(8,128)(2,1)}, u32[]{:S(2)}, u32[]{:S(2)}) collective-permute-start(bf16[768,2048]{1,0:T(8,128)(2,1)} %convolution_convert_fusion), channel_id=1, source_target_pairs={{0,1},{1,0},{2,3},{3,2},{4,5},{5,4},{6,7},{7,6},{8,9},{9,8},{10,11... | collective-permute-start | bytes 9437192 | tf_op jit(solution)/shard_map/ppermute | solution.py:30
  342.7 64.5 %copy-start.17 = (f32[512,384]{1,0:T(8,128)S(1)}, f32[512,384]{1,0:T(8,128)}, u32[]{:S(2)}) copy-start(f32[512,384]{1,0:T(8,128)} %get-tuple-element.155) | copy-start | bytes 2359300
  342.7 64.5 %copy-start.18 = (f32[512,384]{1,0:T(8,128)S(1)}, f32[512,384]{1,0:T(8,128)}, u32[]{:S(2)}) copy-start(f32[512,384]{1,0:T(8,128)} %get-tuple-element.156) | copy-start | bytes 2359300
  343.8 69.7 %collective-permute-start.26 = (bf16[384,1536]{1,0:T(8,128)(2,1)}, bf16[384,1536]{1,0:T(8,128)(2,1)}, u32[]{:S(2)}, u32[]{:S(2)}) collective-permute-start(bf16[384,1536]{1,0:T(8,128)(2,1)} %slice.260), channel_id=1, source_target_pairs={{0,2},{2,0},{1,3},{3,1},{4,6},{6,4},{5,7},{7,5},{8,10},{10,8},{9,1... | collective-permute-start | bytes 3538952 | tf_op jit(solution)/shard_map/ppermute | solution.py:26
  415.3 14.3 %collective-permute-start.27 = (bf16[192,1536]{1,0:T(8,128)(2,1)S(1)}, bf16[192,1536]{1,0:T(8,128)(2,1)S(1)}, u32[]{:S(2)}, u32[]{:S(2)}) collective-permute-start(bf16[192,1536]{1,0:T(8,128)(2,1)S(1)} %broadcast_select_fusion.2), channel_id=1, source_target_pairs={{0,4},{4,0},{8,12},{12,8},{16,20},{20,16},{24,28},{28,24},{1,5},{5... | collective-permute-start | bytes 1769480 | tf_op jit(solution)/shard_map/ppermute | solution.py:238
  420.4 9.4 %copy-start.85 = (bf16[512,1024]{1,0:T(8,128)(2,1)S(1)}, bf16[512,1024]{1,0:T(8,128)(2,1)}, u32[]{:S(2)}) copy-start(bf16[512,1024]{1,0:T(8,128)(2,1)} %copy-done.84) | copy-start | bytes 3145732
  420.5 9.3 %copy-start.47 = (bf16[512,768]{1,0:T(8,128)(2,1)S(1)}, bf16[512,768]{1,0:T(8,128)(2,1)}, u32[]{:S(2)}) copy-start(bf16[512,768]{1,0:T(8,128)(2,1)} %copy-done.45) | copy-start | bytes 2359300
  420.6 29.0 %collective-permute-start.16 = (bf16[384,1536]{1,0:T(8,128)(2,1)S(1)}, bf16[384,1536]{1,0:T(8,128)(2,1)S(1)}, u32[]{:S(2)}, u32[]{:S(2)}) collective-permute-start(bf16[384,1536]{1,0:T(8,128)(2,1)S(1)} %pad_maximum_fusion.10), channel_id=1, source_target_pairs={{0,2},{2,0},{1,3},{3,1},{4,6},{6,4},{5,7},{7,5},{8,10},{10,8},{9,1... | collective-permute-start | bytes 3538952 | tf_op jit(solution)/shard_map/ppermute | solution.py:26
  433.8 63.0 %collective-permute-start.35 = (bf16[384,3072]{1,0:T(8,128)(2,1)S(1)}, bf16[384,3072]{1,0:T(8,128)(2,1)S(1)}, u32[]{:S(2)}, u32[]{:S(2)}) collective-permute-start(bf16[384,3072]{1,0:T(8,128)(2,1)S(1)} %pad_maximum_fusion.1), channel_id=1, source_target_pairs={{0,2},{2,0},{1,3},{3,1},{4,6},{6,4},{5,7},{7,5},{8,10},{10,8},{9,1... | collective-permute-start | bytes 7077896 | tf_op jit(solution)/shard_map/ppermute | solution.py:26
  435.3 15.7 %collective-permute-start.28 = (bf16[96,1536]{1,0:T(8,128)(2,1)S(1)}, bf16[96,1536]{1,0:T(8,128)(2,1)S(1)}, u32[]{:S(2)}, u32[]{:S(2)}) collective-permute-start(bf16[96,1536]{1,0:T(8,128)(2,1)S(1)} %broadcast_select_fusion.5), channel_id=1, source_target_pairs={{0,8},{4,12},{8,0},{12,4},{16,24},{20,28},{24,16},{28,20},{1,9},{5... | collective-permute-start | bytes 884744 | tf_op jit(solution)/shard_map/ppermute | solution.py:238
  449.9 50.0 %collective-permute-start.17 = (bf16[192,1536]{1,0:T(8,128)(2,1)S(1)}, bf16[192,1536]{1,0:T(8,128)(2,1)S(1)}, u32[]{:S(2)}, u32[]{:S(2)}) collective-permute-start(bf16[192,1536]{1,0:T(8,128)(2,1)S(1)} %broadcast_select_fusion.3), channel_id=1, source_target_pairs={{0,4},{4,0},{8,12},{12,8},{16,20},{20,16},{24,28},{28,24},{1,5},{5... | collective-permute-start | bytes 1769480 | tf_op jit(solution)/shard_map/ppermute | solution.py:238
  451.1 48.1 %collective-permute-start.29 = (bf16[48,1536]{1,0:T(8,128)(2,1)S(1)}, bf16[48,1536]{1,0:T(8,128)(2,1)S(1)}, u32[]{:S(2)}, u32[]{:S(2)}) collective-permute-start(bf16[48,1536]{1,0:T(8,128)(2,1)S(1)} %broadcast_select_fusion.7), channel_id=1, source_target_pairs={{0,16},{4,20},{8,24},{12,28},{16,0},{20,4},{24,8},{28,12},{1,17},{... | collective-permute-start | bytes 442376 | tf_op jit(solution)/shard_map/ppermute | solution.py:238
  497.9 24.8 %collective-permute-start.36 = (bf16[192,3072]{1,0:T(8,128)(2,1)S(1)}, bf16[192,3072]{1,0:T(8,128)(2,1)S(1)}, u32[]{:S(2)}, u32[]{:S(2)}) collective-permute-start(bf16[192,3072]{1,0:T(8,128)(2,1)S(1)} %broadcast_select_fusion), channel_id=1, source_target_pairs={{0,4},{4,0},{8,12},{12,8},{16,20},{20,16},{24,28},{28,24},{1,5},{5... | collective-permute-start | bytes 3538952 | tf_op jit(solution)/shard_map/ppermute | solution.py:238
  499.3 54.6 %collective-permute-start.30 = (bf16[48,1536]{1,0:T(8,128)(2,1)S(1)}, bf16[48,1536]{1,0:T(8,128)(2,1)S(1)}, u32[]{:S(2)}, u32[]{:S(2)}) collective-permute-start(bf16[48,1536]{1,0:T(8,128)(2,1)S(1)} %add_convert_fusion.17), channel_id=1, source_target_pairs={{0,16},{4,20},{8,24},{12,28},{16,0},{20,4},{24,8},{28,12},{1,17},{... | collective-permute-start | bytes 442376 | tf_op jit(solution)/shard_map/ppermute | solution.py:244
  500.1 23.8 %collective-permute-start.18 = (bf16[96,1536]{1,0:T(8,128)(2,1)S(1)}, bf16[96,1536]{1,0:T(8,128)(2,1)S(1)}, u32[]{:S(2)}, u32[]{:S(2)}) collective-permute-start(bf16[96,1536]{1,0:T(8,128)(2,1)S(1)} %broadcast_select_fusion.6), channel_id=1, source_target_pairs={{0,8},{4,12},{8,0},{12,4},{16,24},{20,28},{24,16},{28,20},{1,9},{5... | collective-permute-start | bytes 884744 | tf_op jit(solution)/shard_map/ppermute | solution.py:238
  523.4 14.4 %collective-permute-start.37 = (bf16[96,3072]{1,0:T(8,128)(2,1)S(1)}, bf16[96,3072]{1,0:T(8,128)(2,1)S(1)}, u32[]{:S(2)}, u32[]{:S(2)}) collective-permute-start(bf16[96,3072]{1,0:T(8,128)(2,1)S(1)} %broadcast_select_fusion.1), channel_id=1, source_target_pairs={{0,8},{4,12},{8,0},{12,4},{16,24},{20,28},{24,16},{28,20},{1,9},{5... | collective-permute-start | bytes 1769480 | tf_op jit(solution)/shard_map/ppermute | solution.py:238
  524.0 14.1 %collective-permute-start.19 = (bf16[48,1536]{1,0:T(8,128)(2,1)S(1)}, bf16[48,1536]{1,0:T(8,128)(2,1)S(1)}, u32[]{:S(2)}, u32[]{:S(2)}) collective-permute-start(bf16[48,1536]{1,0:T(8,128)(2,1)S(1)} %broadcast_select_fusion.8), channel_id=1, source_target_pairs={{0,16},{4,20},{8,24},{12,28},{16,0},{20,4},{24,8},{28,12},{1,17},{... | collective-permute-start | bytes 442376 | tf_op jit(solution)/shard_map/ppermute | solution.py:238
  538.1 15.6 %collective-permute-start.38 = (bf16[48,3072]{1,0:T(8,128)(2,1)S(1)}, bf16[48,3072]{1,0:T(8,128)(2,1)S(1)}, u32[]{:S(2)}, u32[]{:S(2)}) collective-permute-start(bf16[48,3072]{1,0:T(8,128)(2,1)S(1)} %broadcast_select_fusion.4), channel_id=1, source_target_pairs={{0,16},{4,20},{8,24},{12,28},{16,0},{20,4},{24,8},{28,12},{1,17},{... | collective-permute-start | bytes 884744 | tf_op jit(solution)/shard_map/ppermute | solution.py:238
  538.3 18.6 %collective-permute-start.20 = (bf16[48,1536]{1,0:T(8,128)(2,1)S(1)}, bf16[48,1536]{1,0:T(8,128)(2,1)S(1)}, u32[]{:S(2)}, u32[]{:S(2)}) collective-permute-start(bf16[48,1536]{1,0:T(8,128)(2,1)S(1)} %add_convert_fusion.18), channel_id=1, source_target_pairs={{0,16},{4,20},{8,24},{12,28},{16,0},{20,4},{24,8},{28,12},{1,17},{... | collective-permute-start | bytes 442376 | tf_op jit(solution)/shard_map/ppermute | solution.py:244
  553.8 15.9 %collective-permute-start.39 = (bf16[48,3072]{1,0:T(8,128)(2,1)S(1)}, bf16[48,3072]{1,0:T(8,128)(2,1)S(1)}, u32[]{:S(2)}, u32[]{:S(2)}) collective-permute-start(bf16[48,3072]{1,0:T(8,128)(2,1)S(1)} %add_convert_fusion.14), channel_id=1, source_target_pairs={{0,16},{4,20},{8,24},{12,28},{16,0},{20,4},{24,8},{28,12},{1,17},{... | collective-permute-start | bytes 884744 | tf_op jit(solution)/shard_map/ppermute | solution.py:244
  554.0 17.0 %collective-permute-start.31 = (bf16[96,1536]{1,0:T(8,128)(2,1)S(1)}, bf16[96,1536]{1,0:T(8,128)(2,1)S(1)}, u32[]{:S(2)}, u32[]{:S(2)}) collective-permute-start(bf16[96,1536]{1,0:T(8,128)(2,1)S(1)} %maximum_select_fusion.14), channel_id=1, source_target_pairs={{0,8},{4,12},{8,0},{12,4},{16,24},{20,28},{24,16},{28,20},{1,9},{5... | collective-permute-start | bytes 884744 | tf_op jit(solution)/shard_map/ppermute | solution.py:244
  556.9 20.3 %collective-permute-start.21 = (bf16[96,1536]{1,0:T(8,128)(2,1)S(1)}, bf16[96,1536]{1,0:T(8,128)(2,1)S(1)}, u32[]{:S(2)}, u32[]{:S(2)}) collective-permute-start(bf16[96,1536]{1,0:T(8,128)(2,1)S(1)} %maximum_select_fusion.13), channel_id=1, source_target_pairs={{0,8},{4,12},{8,0},{12,4},{16,24},{20,28},{24,16},{28,20},{1,9},{5... | collective-permute-start | bytes 884744 | tf_op jit(solution)/shard_map/ppermute | solution.py:244
  569.8 19.1 %collective-permute-start.40 = (bf16[96,3072]{1,0:T(8,128)(2,1)S(1)}, bf16[96,3072]{1,0:T(8,128)(2,1)S(1)}, u32[]{:S(2)}, u32[]{:S(2)}) collective-permute-start(bf16[96,3072]{1,0:T(8,128)(2,1)S(1)} %maximum_select_fusion.12), channel_id=1, source_target_pairs={{0,8},{4,12},{8,0},{12,4},{16,24},{20,28},{24,16},{28,20},{1,9},{5... | collective-permute-start | bytes 1769480 | tf_op jit(solution)/shard_map/ppermute | solution.py:244
  571.0 20.0 %collective-permute-start.32 = (bf16[192,1536]{1,0:T(8,128)(2,1)S(1)}, bf16[192,1536]{1,0:T(8,128)(2,1)S(1)}, u32[]{:S(2)}, u32[]{:S(2)}) collective-permute-start(bf16[192,1536]{1,0:T(8,128)(2,1)S(1)} %maximum_select_fusion.11), channel_id=1, source_target_pairs={{0,4},{4,0},{8,12},{12,8},{16,20},{20,16},{24,28},{28,24},{1,5},{5... | collective-permute-start | bytes 1769480 | tf_op jit(solution)/shard_map/ppermute | solution.py:244
  577.4 22.7 %collective-permute-start.22 = (bf16[192,1536]{1,0:T(8,128)(2,1)S(1)}, bf16[192,1536]{1,0:T(8,128)(2,1)}, u32[]{:S(2)}, u32[]{:S(2)}) collective-permute-start(bf16[192,1536]{1,0:T(8,128)(2,1)S(1)} %maximum_select_fusion.10), channel_id=1, source_target_pairs={{0,4},{4,0},{8,12},{12,8},{16,20},{20,16},{24,28},{28,24},{1,5},{5... | collective-permute-start | bytes 1769480 | tf_op jit(solution)/shard_map/ppermute | solution.py:244
  589.2 34.6 %collective-permute-start.41 = (bf16[192,3072]{1,0:T(8,128)(2,1)S(1)}, bf16[192,3072]{1,0:T(8,128)(2,1)S(1)}, u32[]{:S(2)}, u32[]{:S(2)}) collective-permute-start(bf16[192,3072]{1,0:T(8,128)(2,1)S(1)} %maximum_select_fusion.7), channel_id=1, source_target_pairs={{0,4},{4,0},{8,12},{12,8},{16,20},{20,16},{24,28},{28,24},{1,5},{5... | collective-permute-start | bytes 3538952 | tf_op jit(solution)/shard_map/ppermute | solution.py:244
  (68 other events, 198.0 us)
